TPU v7x, 512 devices: a whole 4x8x8 slice. The times are simulated.
512 devices in a mesh: section: 8 (over y), dp: 16 (over z, core), tensor: 4 (over x).
Axes of the slice: x: 4, y: 8, z: 8, core: 2. Of those that a mesh axis runs over, the one named last changes fastest.
Arguments:
- section_inputs: bfloat16 [8, 128, 2560], P('section', 'dp', 'tensor'), may hold values from -40 to 40
- entering: bfloat16 [1, 128, 2560], P(None, 'dp', 'tensor'), may hold values from -40 to 40
- grad_outputs: bfloat16 [8, 128, 2560], P('section', 'dp', 'tensor'), may hold values from -6 to 6
- arriving: bfloat16 [1, 128, 2560], P(None, 'dp', 'tensor'), may hold values from -6 to 6
- live_rows: int32 [1], replicated, may hold values from 64 to 128
- stashed_inputs: bfloat16 [8, 2, 128, 2560], P('section', None, 'dp', 'tensor'), may hold values from -40 to 40
- norm_gain: bfloat16 [8, 2560], P('section', 'tensor'), may hold values from 0.25 to 1.75
- up_weight: bfloat16 [8, 2560, 14336], P('section', 'tensor', 'dp'), may hold values from -0.125 to 0.125
- down_weight: bfloat16 [8, 14336, 2560], P('section', 'dp', 'tensor'), may hold values from -0.046875 to 0.046875
- held_blocks: int32 [8, 4, 16, 6], P('section', 'tensor'), may hold values from 0 to 69, as said below
- held_count: int32 [8, 4, 16], P('section', 'tensor'), may hold values from 1 to 6, as said below
- held_owner: int32 [8, 4, 16, 6], P('section', 'tensor'), may hold values from 0 to 15, as said below
- first_moment: float32 [8, 4, 16, 6, 128, 128], P('section', 'tensor', 'dp'), may hold values from -4 to 4
- second_moment: float32 [8, 4, 16, 6, 128, 128], P('section', 'tensor', 'dp'), may hold values from 0.01 to 1
Outputs:
- section_outputs: bfloat16 [8, 2, 128, 2560], P('section', None, 'dp', 'tensor')
- input_grads: bfloat16 [8, 2, 128, 2560], P('section', None, 'dp', 'tensor')
- first_next: float32 [8, 4, 16, 6, 128, 128], P('section', 'tensor', 'dp')
- second_next: float32 [8, 4, 16, 6, 128, 128], P('section', 'tensor', 'dp')
- update_direction: float32 [8, 4, 16, 6, 128, 128], P('section', 'tensor', 'dp')
Inputs may be any that keep to these rules, and one draw needn't show every extreme that they name: `held_blocks`: A number below 35 names a block of the device's up projection share, row-major over 5 x 7 blocks; the others, less 35, a block of its down projection share, row-major over 7 x 5 blocks. A device's first held_count entries are distinct; later entries are not used. `held_count`: some device of each section and tensor index lists 6 trainable blocks. `held_owner`: the owners of one device's trainable blocks are distinct and never the device itself. Each dp index owns at most 6 blocks of one section and tensor index, and some owns exactly 6.
All inputs are finite; a program needn't handle non-finite values.
Results may differ from a plain program's by a relative error of at most 0.015.
Values may be sent and summed in bfloat16 or wider, within the bound.
A program may use at most 64 MiB of HBM per device.

v0:
```python
import jax
import jax.numpy as jnp
from jax import lax
from jax.sharding import PartitionSpec as P

DW = 2560
BLK = 128


EPSILON = 1e-06


def from_behind(value, axis, steps):
    count = lax.axis_size(axis)
    leading, last = (max(0, -steps), min(count, count - steps))
    return lax.ppermute(value, axis, [(source, source + steps) for source in range(leading, last)])


def normed_product(rows_all, gain_row, up_matrix):
    widened = rows_all.astype(jnp.float32)
    squares = jnp.sum(widened * widened, axis=1)
    normed = (widened * gain_row.astype(jnp.float32)).astype(jnp.bfloat16)
    product = jnp.dot(normed, up_matrix, preferred_element_type=jnp.float32)
    return (normed, squares, product)


def scales_of(squares):
    return lax.rsqrt(squares / DW + EPSILON)


def activate(hidden):
    return (hidden * jax.nn.sigmoid(hidden)).astype(jnp.bfloat16)


def hidden_backward(hidden, act_grad, row_scales, product):
    sigmoid_part = jax.nn.sigmoid(hidden)
    hidden_grad = act_grad * sigmoid_part * (1.0 + hidden * (1.0 - sigmoid_part))
    scaled_grad = (hidden_grad * row_scales[:, None]).astype(jnp.bfloat16)
    scale_grad = jnp.sum(hidden_grad * product, axis=1)
    return (scaled_grad, scale_grad)


def times_transposed(left, right):
    return lax.dot_general(
        left, right, (((1,), (1,)), ((), ())), preferred_element_type=jnp.float32
    )


def body(
    section_inputs,
    entering,
    grad_outputs,
    arriving,
    live_rows,
    stashed_inputs,
    norm_gain,
    up_weight,
    down_weight,
    held_blocks,
    held_count,
    held_owner,
    first_moment,
    second_moment,
):
    section_count = lax.axis_size("section")
    section_index = lax.axis_index("section")
    dp_index = lax.axis_index("dp")
    dp_count = lax.axis_size("dp")
    turn_count = stashed_inputs.shape[1]
    local_rows = section_inputs.shape[1]
    row_total = local_rows * dp_count
    gain_row = norm_gain[0]
    up_matrix = up_weight[0]
    down_matrix = down_weight[0]
    channel_blocks = up_matrix.shape[0] // BLK
    hidden_blocks = up_matrix.shape[1] // BLK
    up_count = channel_blocks * hidden_blocks
    capacity = held_owner.shape[3]
    row_start = dp_index * local_rows
    held_list = lax.dynamic_index_in_dim(held_blocks[0, 0], dp_index, 0, keepdims=False)
    down_number = held_list - up_count
    is_up = held_list < up_count
    left_index = jnp.where(
        is_up, held_list // hidden_blocks, channel_blocks + down_number // channel_blocks
    )
    right_index = jnp.where(
        is_up, held_list % hidden_blocks, hidden_blocks + down_number % channel_blocks
    )
    forward_results = []
    rows_in = section_inputs[0]
    for turn in range(turn_count):
        if turn > 0:
            passed_rows = from_behind(forward_results[-1], "section", 1)
            rows_in = jnp.where(section_index == 0, entering[turn - 1], passed_rows)
        forward_rows_all = lax.all_gather(rows_in, "dp", axis=0, tiled=True)
        forward_normed, forward_squares, forward_product = normed_product(
            forward_rows_all, gain_row, up_matrix
        )
        forward_product, forward_squares = (
            lax.psum(forward_product.astype(jnp.bfloat16), "tensor").astype(jnp.float32),
            lax.psum(forward_squares.astype(jnp.bfloat16), "tensor").astype(jnp.float32),
        )
        forward_activated = activate(forward_product * scales_of(forward_squares)[:, None])
        mixed_rows = lax.psum_scatter(
            jnp.dot(forward_activated, down_matrix, preferred_element_type=jnp.float32).astype(
                jnp.bfloat16
            ),
            "dp",
            scatter_dimension=0,
            tiled=True,
        ).astype(jnp.float32)
        forward_results.append((rows_in.astype(jnp.float32) + mixed_rows).astype(jnp.bfloat16))
    row_ids = row_start + lax.iota(jnp.int32, local_rows)
    backward_results = []
    kept_grads = jnp.zeros((capacity, BLK, BLK), jnp.float32)
    grads_in = grad_outputs[0]
    for turn in range(turn_count):
        if turn > 0:
            passed_grads = from_behind(backward_results[-1], "section", -1)
            masked = jnp.where(
                (row_ids < live_rows[turn - 1])[:, None],
                arriving[turn - 1],
                jnp.zeros_like(arriving[turn - 1]),
            )
            grads_in = jnp.where(section_index == section_count - 1, masked, passed_grads)
        rows_local = stashed_inputs[0, turn]
        rows_all = lax.all_gather(rows_local, "dp", axis=0, tiled=True)
        grads_all = lax.all_gather(grads_in, "dp", axis=0, tiled=True)
        normed, squares, product = normed_product(rows_all, gain_row, up_matrix)
        act_grad = times_transposed(grads_all, down_matrix)
        product, squares, act_grad = lax.psum((product, squares, act_grad), "tensor")
        row_scales = scales_of(squares)
        hidden = product * row_scales[:, None]
        activated = activate(hidden)
        scaled_grad, scale_grad = hidden_backward(hidden, act_grad, row_scales, product)
        normed_part = times_transposed(scaled_grad, up_matrix)
        normed_grad = lax.psum_scatter(normed_part, "dp", scatter_dimension=0, tiled=True)
        scale_grad_rows = lax.psum_scatter(scale_grad, "dp", scatter_dimension=0, tiled=True)
        scale_rows = lax.dynamic_slice_in_dim(row_scales, row_start, local_rows, 0)
        widened = rows_local.astype(jnp.float32)
        input_grad = (
            grads_in.astype(jnp.float32)
            + normed_grad * gain_row.astype(jnp.float32)
            - (scale_grad_rows * scale_rows**3)[:, None] * widened / DW
        )
        left_table = jnp.concatenate(
            [
                normed.reshape(row_total, channel_blocks, BLK),
                activated.reshape(row_total, hidden_blocks, BLK),
            ],
            axis=1,
        )
        right_table = jnp.concatenate(
            [
                scaled_grad.reshape(row_total, hidden_blocks, BLK),
                grads_all.reshape(row_total, channel_blocks, BLK),
            ],
            axis=1,
        )
        left_pick = jnp.take(left_table, left_index, axis=1)
        right_pick = jnp.take(right_table, right_index, axis=1)
        block_grads = jnp.einsum(
            "rkb,rkc->kbc", left_pick, right_pick, preferred_element_type=jnp.float32
        )
        result, block_grads = (input_grad.astype(jnp.bfloat16), block_grads)
        backward_results.append(result)
        kept_grads = kept_grads + block_grads
    counts = held_count[0, 0]
    owners = held_owner[0, 0]
    slot_ids = lax.iota(jnp.int32, capacity)
    dp_ids = lax.iota(jnp.int32, dp_count)
    live_slots = slot_ids[None, :] < counts[:, None]
    chosen = (owners[:, None, :] == dp_ids[None, :, None]) & live_slots[:, None, :]
    is_sent = jnp.any(chosen, axis=2)
    slot_pick = jnp.sum(jnp.where(chosen, slot_ids[None, None, :], 0), axis=2)
    mine_sent = lax.dynamic_index_in_dim(is_sent, dp_index, 0, keepdims=False)
    mine_pick = lax.dynamic_index_in_dim(slot_pick, dp_index, 0, keepdims=False)
    outgoing = jnp.where(mine_sent[:, None, None], jnp.take(kept_grads, mine_pick, axis=0), 0.0)
    arrived = lax.all_to_all(outgoing, "dp", split_axis=0, concat_axis=0, tiled=True)
    from_source = lax.dynamic_index_in_dim(is_sent, dp_index, 1, keepdims=False)
    source_count = from_source.astype(jnp.int32)
    ranks = jnp.cumsum(source_count) - source_count
    matches = from_source[None, :] & (ranks[None, :] == slot_ids[:, None])
    is_filled = jnp.any(matches, axis=1)
    source_ids = jnp.sum(jnp.where(matches, dp_ids[None, :], 0), axis=1)
    owned_grads = jnp.where(is_filled[:, None, None], jnp.take(arrived, source_ids, axis=0), 0.0)
    filled = is_filled[:, None, None]
    first_new = 0.9 * first_moment[0, 0, 0] + 0.1 * owned_grads
    second_new = 0.999 * second_moment[0, 0, 0] + 0.001 * owned_grads * owned_grads
    direction = first_new / (jnp.sqrt(second_new) + 1e-08)
    first_out = jnp.where(filled, first_new, 0.0)
    second_out = jnp.where(filled, second_new, 0.0)
    direction_out = jnp.where(filled, direction, 0.0)
    section_rows = jnp.stack(forward_results)
    grad_rows = jnp.stack(backward_results)
    return (
        section_rows[None],
        grad_rows[None],
        first_out[None, None, None],
        second_out[None, None, None],
        direction_out[None, None, None],
    )


def solution(mesh):
    return jax.shard_map(
        body,
        mesh=mesh,
        in_specs=(
            P("section", "dp", "tensor"),
            P(None, "dp", "tensor"),
            P("section", "dp", "tensor"),
            P(None, "dp", "tensor"),
            P(),
            P("section", None, "dp", "tensor"),
            P("section", "tensor"),
            P("section", "tensor", "dp"),
            P("section", "dp", "tensor"),
            P("section", "tensor", None, None),
            P("section", "tensor", None),
            P("section", "tensor", None, None),
            P("section", "tensor", "dp", None, None, None),
            P("section", "tensor", "dp", None, None, None),
        ),
        out_specs=(
            P("section", None, "dp", "tensor"),
            P("section", None, "dp", "tensor"),
            P("section", "tensor", "dp", None, None, None),
            P("section", "tensor", "dp", None, None, None),
            P("section", "tensor", "dp", None, None, None),
        ),
        check_vma=False,
    )
```

profile of v0, /device:TPU:1, one launch (start us, length us, event | category | flops | bytes accessed | tf_op | source)
XLA Modules:
  0.0 778.5 jit_solution(2961250332882547614)
XLA Ops:
  7.2 0.8 convert_reduce_fusion
  8.1 0.7 fusion.77
  8.8 24.9 %all-gather.2 = bf16[1,1,128,640]{3,2,1,0:T(8,128)(2,1)S(1)} all-gather(bf16[1,1,8,640]{3,2,1,0:T(8,128)(2,1)S(1)} %get-tuple-element.41), channel_id=4, replica_groups=mesh['section'=8,'dp'=16,'tensor'=4] {'dp'}, dimensions={2}, use_global_device_ids=true | all-gather | bytes 174080 | tf_op jit(solution)/shard_map/all_gather | solution.py:127
  33.9 15.2 %all-gather.1 = bf16[1,128,640]{2,1,0:T(8,128)(2,1)S(1)} all-gather(bf16[1,8,640]{2,1,0:T(8,128)(2,1)} %param.18), channel_id=3, replica_groups=mesh['section'=8,'dp'=16,'tensor'=4] {'dp'}, dimensions={1}, use_global_device_ids=true | all-gather | bytes 174080 | tf_op jit(solution)/shard_map/all_gather | solution.py:128
  49.0 16.2 %all-gather.3 = bf16[1,1,128,640]{3,2,1,0:T(8,128)(2,1)S(1)} all-gather(bf16[1,1,8,640]{3,2,1,0:T(8,128)(2,1)S(1)} %get-tuple-element.42), channel_id=5, replica_groups=mesh['section'=8,'dp'=16,'tensor'=4] {'dp'}, dimensions={2}, use_global_device_ids=true | all-gather | bytes 174080 | tf_op jit(solution)/shard_map/all_gather | solution.py:127
  65.4 1.2 fusion.2
  66.8 1.2 fusion.12
  68.1 14.9 %all-gather = bf16[1,128,640]{2,1,0:T(8,128)(2,1)S(1)} all-gather(bf16[1,8,640]{2,1,0:T(8,128)(2,1)S(1)} %copy-done.15), channel_id=2, replica_groups=mesh['section'=8,'dp'=16,'tensor'=4] {'dp'}, dimensions={1}, use_global_device_ids=true | all-gather | bytes 174080 | tf_op jit(solution)/shard_map/all_gather | solution.py:95
  83.2 8.9 %all-reduce.6 = (f32[128]{0:T(128)S(1)}, f32[128]{0:T(128)S(1)}) all-reduce(f32[128]{0:T(128)S(1)} %get-tuple-element.38, f32[128]{0:T(128)S(1)} %get-tuple-element.43), channel_id=1, replica_groups=mesh['section'=8,'dp'=16,'tensor'=4] {'tensor'}, use_global_device_ids=true, to_apply=%region_18.19 | all-reduce | flops 256 | bytes 2048 | tf_op jit(solution)/shard_map/psum | solution.py:131
  92.1 27.8 %all-reduce.32.cloned.1.call-done = (f32[128,896]{1,0:T(8,128)}, f32[128,896]{1,0:T(8,128)}) async-done(((f32[128,896]{1,0:T(8,128)}, f32[128,896]{1,0:T(8,128)}), (f32[128,896]{1,0:T(8,128)}, f32[128,896]{1,0:T(8,128)})) %all-reduce.32.cloned.1.call-update) | async-done | bytes 917520 | tf_op jit(solution)/shard_map/psum | solution.py:131
  119.9 1.6 multiply_reduce_fusion.1
  121.4 1.2 fusion.10
  122.7 1.3 convolution_convert_fusion.1
  124.6 0.6 divide_reduce_fusion.1
  126.4 0.6 fusion.65
  129.6 8.1 %psum.71 = bf16[128]{0:T(256)(128)(2,1)S(1)} all-reduce(bf16[128]{0:T(256)(128)(2,1)S(1)} %fusion.21), channel_id=1, replica_groups=mesh['section'=8,'dp'=16,'tensor'=4] {'tensor'}, use_global_device_ids=true, to_apply=%region_2.3 | all-reduce | flops 128 | bytes 512 | tf_op jit(solution)/shard_map/psum | solution.py:101
  137.6 1.2 fusion.8
  138.8 1.3 dynamic-slice.1
  140.8 28.0 %all-reduce.3 = f32[128]{0:T(128)S(1)} all-reduce(f32[128]{0:T(128)S(1)} %get-tuple-element.30), channel_id=9, replica_groups=mesh['section'=8,'dp'=16,'tensor'=4] {'dp'}, use_global_device_ids=true, to_apply=%region_14.15.clone | all-reduce | flops 128 | bytes 1024
  168.9 69.6 %all-reduce.26.cloned.1.call-done = f32[128,640]{1,0:T(8,128)} async-done(((f32[128,640]{1,0:T(8,128)}), f32[128,640]{1,0:T(8,128)}) %all-reduce.26.cloned.1.call-update) | async-done | bytes 327696
  238.6 0.8 fusion.58
  239.4 1.4 collective-permute-start.1
  240.8 50.0 %all-reduce.18.cloned.1.call-done = bf16[128,896]{1,0:T(8,128)(2,1)} async-done(((bf16[128,896]{1,0:T(8,128)(2,1)}), bf16[128,896]{1,0:T(8,128)(2,1)}) %all-reduce.18.cloned.1.call-update) | async-done | bytes 229392 | tf_op jit(solution)/shard_map/psum | solution.py:100
  290.8 2.0 convolution_convert_fusion.3
  293.0 21.1 %all_gather.22 = bf16[128,640]{1,0:T(8,128)(2,1)S(1)} all-gather(bf16[8,640]{1,0:T(8,128)(2,1)S(1)} %fusion.63), channel_id=1, replica_groups=mesh['section'=8,'dp'=16,'tensor'=4] {'dp'}, dimensions={0}, use_global_device_ids=true | all-gather | bytes 174080 | tf_op jit(solution)/shard_map/all_gather | solution.py:128
  314.1 0.7 copy-done.2
  314.8 1.3 fusion
  316.0 88.5 %all-reduce.22.cloned.1.call-done = bf16[128,640]{1,0:T(8,128)(2,1)} async-done(((bf16[128,640]{1,0:T(8,128)(2,1)}), bf16[128,640]{1,0:T(8,128)(2,1)}) %all-reduce.22.cloned.1.call-update) | async-done | bytes 163856
  404.6 0.7 fusion.59
  405.3 3.1 collective-permute-start
  409.1 0.8 copy.104
  410.0 0.8 copy.99
  410.8 0.8 copy.107
  411.6 16.2 %all_gather.19 = bf16[128,640]{1,0:T(8,128)(2,1)S(1)} all-gather(bf16[8,640]{1,0:T(8,128)(2,1)S(1)} %bitcast_select_fusion.2), channel_id=1, replica_groups=mesh['section'=8,'dp'=16,'tensor'=4] {'dp'}, dimensions={0}, use_global_device_ids=true | all-gather | bytes 174080 | tf_op jit(solution)/shard_map/all_gather | solution.py:95
  428.4 0.8 copy.100
  429.4 1.1 pad_maximum_fusion
  431.1 1.0 pad_maximum_fusion.1
  433.2 0.8 copy.112
  434.0 26.0 %all-reduce.30.cloned.1.call-done = (f32[128,896]{1,0:T(8,128)}, f32[128,896]{1,0:T(8,128)}) async-done(((f32[128,896]{1,0:T(8,128)}, f32[128,896]{1,0:T(8,128)}), (f32[128,896]{1,0:T(8,128)}, f32[128,896]{1,0:T(8,128)})) %all-reduce.30.cloned.1.call-update) | async-done | bytes 917520 | tf_op jit(solution)/shard_map/psum | solution.py:131
  460.1 2.1 multiply_reduce_fusion
  462.4 0.8 copy.108
  463.2 1.1 pad_maximum_fusion.2
  464.3 1.4 gather_fusion.4
  465.8 0.8 copy.111
  466.7 1.1 pad_maximum_fusion.3
  467.7 1.4 gather_fusion.5
  469.1 1.4 convolution_add_fusion
  470.5 1.8 gather_fusion
  472.3 2.5 select_select_fusion
  474.7 9.7 %all-to-all-start = ((f32[16,128,128]{2,1,0:T(8,128)}), f32[16,128,128]{2,1,0:T(8,128)}, u32[]{:S(2)}, u32[]{:S(2)}) async-start(f32[16,128,128]{2,1,0:T(8,128)} %select_select_fusion), calls=%async_computation | async-start | bytes 2097152 | tf_op jit(solution)/shard_map/all_to_all | solution.py:179
  484.5 1.3 convolution_convert_fusion
  485.9 8.5 %psum.73 = bf16[128]{0:T(256)(128)(2,1)S(1)} all-reduce(bf16[128]{0:T(256)(128)(2,1)S(1)} %fusion.19), channel_id=1, replica_groups=mesh['section'=8,'dp'=16,'tensor'=4] {'tensor'}, use_global_device_ids=true, to_apply=%region_6.7 | all-reduce | flops 128 | bytes 512 | tf_op jit(solution)/shard_map/psum | solution.py:101
  494.4 43.6 %all-reduce.20.cloned.1.call-done = bf16[128,896]{1,0:T(8,128)(2,1)} async-done(((bf16[128,896]{1,0:T(8,128)(2,1)}), bf16[128,896]{1,0:T(8,128)(2,1)}) %all-reduce.20.cloned.1.call-update) | async-done | bytes 229392 | tf_op jit(solution)/shard_map/psum | solution.py:100
  538.1 2.0 convolution_convert_fusion.2
  540.2 111.8 %all-reduce.24.cloned.1.call-done = bf16[128,640]{1,0:T(8,128)(2,1)} async-done(((bf16[128,640]{1,0:T(8,128)(2,1)}), bf16[128,640]{1,0:T(8,128)(2,1)}) %all-reduce.24.cloned.1.call-update) | async-done | bytes 163856
  652.0 0.7 fusion.61
  652.7 1.2 fusion.6
  654.0 0.6 maximum_bitcast_fusion
  654.6 23.2 %all-reduce.5 = f32[128]{0:T(128)S(1)} all-reduce(f32[128]{0:T(128)S(1)} %copy-done.28), channel_id=11, replica_groups=mesh['section'=8,'dp'=16,'tensor'=4] {'dp'}, use_global_device_ids=true, to_apply=%region_21.22.clone | all-reduce | flops 128 | bytes 1024
  677.8 89.3 %all-reduce.28.cloned.1.call-done = f32[128,640]{1,0:T(8,128)} async-done(((f32[128,640]{1,0:T(8,128)}), f32[128,640]{1,0:T(8,128)}) %all-reduce.28.cloned.1.call-update) | async-done | bytes 327696
  767.1 0.8 fusion.62
  767.9 0.6 maximum_bitcast_fusion.1
  768.5 1.8 gather_fusion.1
  770.4 1.3 divide_select_fusion
  (133 shorter events, 8.7 us)
Async XLA Ops:
  7.2 59.6 %copy-start = (bf16[1,640,896]{2,1,0:T(8,128)(2,1)S(1)}, bf16[1,640,896]{2,1,0:T(8,128)(2,1)}, u32[]{:S(2)}) copy-start(bf16[1,640,896]{2,1,0:T(8,128)(2,1)} %param.23) | copy-start | bytes 3440644
  7.2 58.2 %copy-start.1 = (bf16[1,896,640]{2,1,0:T(8,128)(2,1)S(1)}, bf16[1,896,640]{2,1,0:T(8,128)(2,1)}, u32[]{:S(2)}) copy-start(bf16[1,896,640]{2,1,0:T(8,128)(2,1)} %param.24) | copy-start | bytes 3440644
  7.2 112.7 %all-reduce.32.cloned.1.call-start = ((), (), s32[]{:S(2)}) async-start(), calls=%async_computation.8 | async-start | bytes 1835008 | tf_op jit(solution)/shard_map/psum | solution.py:131
  66.8 1.3 copy-start.15
  68.0 170.5 %all-reduce.26.cloned.1.call-start = ((), (), s32[]{:S(2)}) async-start(), calls=%async_computation.5 | async-start | bytes 655360
  122.6 1.4 copy-start.16
  122.6 2.5 copy-start.34
  122.6 2.6 copy-start.25
  122.7 168.1 %all-reduce.18.cloned.1.call-start = ((), (), s32[]{:S(2)}) async-start(), calls=%async_computation.1 | async-start | bytes 458752 | tf_op jit(solution)/shard_map/psum | solution.py:100
  124.0 114.6 %copy-start.8 = (bf16[1,2,8,640]{3,2,1,0:T(8,128)(2,1)S(1)}, bf16[1,2,8,640]{3,2,1,0:T(8,128)(2,1)}, u32[]{:S(2)}) copy-start(bf16[1,2,8,640]{3,2,1,0:T(8,128)(2,1)} %param.21) | copy-start | bytes 61444
  124.0 114.6 %copy-start.14 = (bf16[1,8,640]{2,1,0:T(8,128)(2,1)S(1)}, bf16[1,8,640]{2,1,0:T(8,128)(2,1)}, u32[]{:S(2)}) copy-start(bf16[1,8,640]{2,1,0:T(8,128)(2,1)} %param.18) | copy-start | bytes 30724
  124.0 280.6 %all-reduce.22.cloned.1.call-start = ((), (), s32[]{:S(2)}) async-start(), calls=%async_computation.3 | async-start | bytes 327680
  129.6 330.5 %copy-start.26 = (f32[128]{0:T(128)}, f32[128]{0:T(128)S(1)}, u32[]{:S(2)}) copy-start(f32[128]{0:T(128)S(1)} %add_rsqrt_fusion) | copy-start | bytes 1540
  140.8 291.9 %copy-start.21 = (pred[6]{0:T(512)(128)(4,1)}, pred[6]{0:T(512)(128)(4,1)S(1)}, u32[]{:S(2)}) copy-start(pred[6]{0:T(512)(128)(4,1)S(1)} %get-tuple-element.24) | copy-start | bytes 22
  140.8 291.9 %copy-start.23 = (pred[6]{0:T(512)(128)(4,1)}, pred[6]{0:T(512)(128)(4,1)S(1)}, u32[]{:S(2)}) copy-start(pred[6]{0:T(512)(128)(4,1)S(1)} %get-tuple-element.47) | copy-start | bytes 22
  140.8 289.7 %copy-start.20 = (s32[1024]{0:T(1024)}, s32[1024]{0:T(1024)S(1)}, u32[]{:S(2)}) copy-start(s32[1024]{0:T(1024)S(1)} %get-tuple-element.50) | copy-start | bytes 12292
  140.8 291.3 %copy-start.19 = (s32[1024]{0:T(1024)}, s32[1024]{0:T(1024)S(1)}, u32[]{:S(2)}) copy-start(s32[1024]{0:T(1024)S(1)} %get-tuple-element.49) | copy-start | bytes 12292
  239.4 53.5 %copy-start.10 = (bf16[8,640]{1,0:T(8,128)(2,1)}, bf16[8,640]{1,0:T(8,128)(2,1)S(1)}, u32[]{:S(2)}) copy-start(bf16[8,640]{1,0:T(8,128)(2,1)S(1)} %fusion.58) | copy-start | bytes 30724
  239.4 53.5 %copy-start.17 = (bf16[1,8,640]{2,1,0:T(8,128)(2,1)S(1)}, bf16[1,8,640]{2,1,0:T(8,128)(2,1)}, u32[]{:S(2)}) copy-start(bf16[1,8,640]{2,1,0:T(8,128)(2,1)} %param.19) | copy-start | bytes 30724
  239.4 53.5 %collective-permute-start.1 = (bf16[8,640]{1,0:T(8,128)(2,1)S(1)}, bf16[8,640]{1,0:T(8,128)(2,1)S(1)}, u32[]{:S(2)}, u32[]{:S(2)}) collective-permute-start(bf16[8,640]{1,0:T(8,128)(2,1)S(1)} %fusion.58), channel_id=1, source_target_pairs={{64,0},{128,64},{192,128},{256,192},{320,256},{384,320},{448,384},... | collective-permute-start | bytes 30728 | tf_op jit(solution)/shard_map/ppermute | solution.py:16
  292.8 167.2 %all-reduce.30.cloned.1.call-start = ((), (), s32[]{:S(2)}) async-start(), calls=%async_computation.7 | async-start | bytes 1835008 | tf_op jit(solution)/shard_map/psum | solution.py:131
  314.1 0.7 copy-start.2
  316.0 95.6 %copy-start.18 = (bf16[1,8,640]{2,1,0:T(8,128)(2,1)S(1)}, bf16[1,8,640]{2,1,0:T(8,128)(2,1)}, u32[]{:S(2)}) copy-start(bf16[1,8,640]{2,1,0:T(8,128)(2,1)} %param.17) | copy-start | bytes 30724
  405.3 6.3 copy-start.12
  405.3 6.3 collective-permute-start
  411.6 17.6 %copy-start.6 = (bf16[8,640]{1,0:T(8,128)(2,1)}, bf16[8,640]{1,0:T(8,128)(2,1)S(1)}, u32[]{:S(2)}) copy-start(bf16[8,640]{1,0:T(8,128)(2,1)S(1)} %bitcast_select_fusion.2) | copy-start | bytes 30724
  431.1 2.0 copy-start.3
  465.6 3.5 copy-start.22
  465.6 3.5 copy-start.24
  470.5 1.8 copy-start.32
  470.5 1.8 copy-start.33
  474.7 293.8 %all-to-all-start = ((f32[16,128,128]{2,1,0:T(8,128)}), f32[16,128,128]{2,1,0:T(8,128)}, u32[]{:S(2)}, u32[]{:S(2)}) async-start(f32[16,128,128]{2,1,0:T(8,128)} %select_select_fusion), calls=%async_computation | async-start | bytes 2097152 | tf_op jit(solution)/shard_map/all_to_all | solution.py:179
  484.4 53.7 %all-reduce.20.cloned.1.call-start = ((), (), s32[]{:S(2)}) async-start(), calls=%async_computation.2 | async-start | bytes 458752 | tf_op jit(solution)/shard_map/psum | solution.py:100
  485.7 166.3 %all-reduce.24.cloned.1.call-start = ((), (), s32[]{:S(2)}) async-start(), calls=%async_computation.4 | async-start | bytes 327680
  494.4 45.8 %copy-start.29 = (s32[6]{0:T(128)S(1)}, s32[6]{0:T(128)}, u32[]{:S(2)}) copy-start(s32[6]{0:T(128)} %fusion.72) | copy-start | bytes 76
  494.4 157.6 %copy-start.7 = (bf16[8,640]{1,0:T(8,128)(2,1)S(1)}, bf16[8,640]{1,0:T(8,128)(2,1)}, u32[]{:S(2)}) copy-start(bf16[8,640]{1,0:T(8,128)(2,1)} %copy-done.6) | copy-start | bytes 30724
  540.1 113.8 %copy-start.13 = (bf16[8,640]{1,0:T(8,128)(2,1)S(1)}, bf16[8,640]{1,0:T(8,128)(2,1)}, u32[]{:S(2)}) copy-start(bf16[8,640]{1,0:T(8,128)(2,1)} %copy-done.12) | copy-start | bytes 30724
  540.1 114.5 %copy-start.28 = (f32[128]{0:T(128)S(1)}, f32[128]{0:T(128)}, u32[]{:S(2)}) copy-start(f32[128]{0:T(128)} %get-tuple-element.28) | copy-start | bytes 1540
  540.1 137.6 %copy-start.27 = (f32[128]{0:T(128)S(1)}, f32[128]{0:T(128)}, u32[]{:S(2)}) copy-start(f32[128]{0:T(128)} %copy-done.26) | copy-start | bytes 1540
  540.1 227.0 %copy-start.9 = (bf16[1,2,8,640]{3,2,1,0:T(8,128)(2,1)S(1)}, bf16[1,2,8,640]{3,2,1,0:T(8,128)(2,1)}, u32[]{:S(2)}) copy-start(bf16[1,2,8,640]{3,2,1,0:T(8,128)(2,1)} %param.21) | copy-start | bytes 61444
  540.1 227.8 %copy-start.11 = (bf16[8,640]{1,0:T(8,128)(2,1)S(1)}, bf16[8,640]{1,0:T(8,128)(2,1)}, u32[]{:S(2)}) copy-start(bf16[8,640]{1,0:T(8,128)(2,1)} %copy-done.10) | copy-start | bytes 30724
  540.2 226.9 %all-reduce.28.cloned.1.call-start = ((), (), s32[]{:S(2)}) async-start(), calls=%async_computation.6 | async-start | bytes 655360
  652.7 117.6 %copy-start.4 = (f32[1,1,1,6,128,128]{5,4,3,2,1,0:T(8,128)S(1)}, f32[1,1,1,6,128,128]{5,4,3,2,1,0:T(8,128)}, u32[]{:S(2)}) copy-start(f32[1,1,1,6,128,128]{5,4,3,2,1,0:T(8,128)} %param.28) | copy-start | bytes 1179652
  652.7 117.6 %copy-start.5 = (f32[1,1,1,6,128,128]{5,4,3,2,1,0:T(8,128)S(1)}, f32[1,1,1,6,128,128]{5,4,3,2,1,0:T(8,128)}, u32[]{:S(2)}) copy-start(f32[1,1,1,6,128,128]{5,4,3,2,1,0:T(8,128)} %param.29) | copy-start | bytes 1179652
  652.7 117.6 %copy-start.30 = (pred[6]{0:T(512)(128)(4,1)S(1)}, pred[6]{0:T(512)(128)(4,1)}, u32[]{:S(2)}) copy-start(pred[6]{0:T(512)(128)(4,1)} %fusion.65) | copy-start | bytes 22
  652.7 117.6 %copy-start.31 = (pred[6]{0:T(512)(128)(4,1)S(1)}, pred[6]{0:T(512)(128)(4,1)}, u32[]{:S(2)}) copy-start(pred[6]{0:T(512)(128)(4,1)} %compare_and_fusion.3) | copy-start | bytes 22
Sparse Core Ops, SparseCore 0:
  68.2 51.6 all-reduce.31
  122.8 115.7 all-reduce.25
  241.6 49.1 all-reduce.17
  293.5 110.9 all-reduce.21
  406.9 53.0 all-reduce.29
  487.9 50.0 all-reduce.19
  541.0 110.9 all-reduce.23
  655.0 112.0 all-reduce.27
where the time goes:
time: 779 us; the launch traced here: 778 us
  waiting for transfers between devices  507 us (65%)
  blocking collectives  185 us (24%)
  other arithmetic  22 us (3%)
  local copies, waits for them, and re-layouts  18.4 us (2%)
  between operations  16 us (2%)
  matrix products  15.5 us (2%)
  starting transfers between devices  14.6 us (2%)
    unnamed x12, waiting for transfers between devices  359 us
    psum x2, waiting for transfers between devices, body(): lax.psum(forward_product.astype(jnp.bfloat16), 'tensor').astype(jnp.float32)  93.6 us
    psum x2, waiting for transfers between devices, body(): lax.psum((product, squares, act_grad), 'tensor')  53.8 us
    unnamed x2, blocking collectives  51.2 us
    all_gather x2, blocking collectives, body(): rows_all = lax.all_gather(rows_local, 'dp', axis=0, tiled=True)  41.1 us
    all_gather x2, blocking collectives, body(): grads_all = lax.all_gather(grads_in, 'dp', axis=0, tiled=True)  36.3 us
    all_gather x2, blocking collectives, body(): forward_rows_all = lax.all_gather(rows_in, 'dp', axis=0, tiled=True)  31.2 us
    psum x2, blocking collectives, body(): lax.psum(forward_squares.astype(jnp.bfloat16), 'tensor').astype(jnp.float32)  16.6 us
  transfers between devices with their start and end apart: 11, of which 8 were waited for; matrix products, arithmetic and copies ran while one was open for 4% of the time, Pallas kernels for 0%

commit v1 on v0

v1 whole, which is shorter than its diff:
```python
import functools

import jax
import jax.numpy as jnp
from jax import lax
from jax.experimental import pallas as pl
from jax.experimental.pallas import tpu as pltpu
from jax.sharding import PartitionSpec as P

MESH = pl.DeviceIdType.MESH
BLK = 128
LANES = 128
EPSILON = 1e-06
F32 = jnp.float32
BF16 = jnp.bfloat16


def times_transposed(left, right):
    return lax.dot_general(left, right, (((1,), (1,)), ((), ())), preferred_element_type=F32)


def lane_blocks_sum(value):
    total = value[:, :LANES]
    for start in range(LANES, value.shape[1], LANES):
        total = total + value[:, start : start + LANES]
    return total


def kernel(
    sizes,
    live_ref, blocks_ref, count_ref, owner_ref,
    section_ref, entering_ref, grad_ref, arriving_ref, stash_ref, gain_ref,
    up_hbm, down_hbm,
    outputs_ref, grads_ref, owned_ref, filled_ref,
    up_ref, down_ref,
    src_a, src_b, all_a, all_b, src_f, src_d, all_f, all_d,
    sent_p0, sent_a0, sent_f0, sent_p1, sent_a1, sent_f1,
    got_p0, got_a0, got_f0, got_p1, got_a1, got_f1,
    mix_s0, mix_h0, mix_f0, mix_h1, mix_s1, mix_f1,
    keep_b0, keep_f0, keep_b1, keep_f1,
    half_b0, half_f0, half_b1, half_f1,
    other_b0, other_f0, other_b1, other_f1,
    chip_b0, chip_f0, chip_b1, chip_f1,
    rows_b0, rows_f0, rows_b1, rows_f1,
    left_table, right_table, block_buf, send_buf, recv_buf,
    held_p1, held_scale1,
    weight_sem,
    gather_send, gather_recv,
    tensor_send, tensor_recv,
    reduce_send, reduce_recv,
    block_send, block_recv,
):
    ns, nz, nt = sizes
    nd = 2 * nz
    local, width = section_ref.shape
    hidden = up_ref.shape[1]
    rows = local * nd
    part = rows // nt
    dw = width * nt
    section = lax.axis_index("section")
    dp = lax.axis_index("dp")
    tensor = lax.axis_index("tensor")
    z = dp // 2
    core = dp % 2
    partner = (section, z * 2 + 1 - core, tensor)
    after = lax.rem(section + 1, ns)
    before = lax.rem(section + ns - 1, ns)

    def remote(src, dst, send_sem, recv_sem, device):
        return pltpu.make_async_remote_copy(
            src_ref=src, dst_ref=dst, send_sem=send_sem, recv_sem=recv_sem,
            device_id=device, device_id_type=MESH,
        )

    def far_first(k):
        return nz // 2 + (1 - 2 * (k % 2)) * ((k + 1) // 2)

    def zup(j):
        return lax.rem(z + j, nz)

    def zdown(j):
        return lax.rem(z + nz - j, nz)

    def tup(j):
        return lax.rem(tensor + j, nt)

    def loop(lo, hi, fn):
        def step(k, carry):
            fn(k)
            return carry
        lax.fori_loop(lo, hi, step, 0)

    weights_up = pltpu.make_async_copy(up_hbm, up_ref, weight_sem.at[0])
    weights_down = pltpu.make_async_copy(down_hbm, down_ref, weight_sem.at[1])
    weights_up.start()
    weights_down.start()

    barrier = pltpu.get_barrier_semaphore()

    def greet(device):
        pl.semaphore_signal(barrier, inc=1, device_id=device, device_id_type=MESH)

    def greet_dp(k):
        greet((section, lax.rem(dp + k, nd), tensor))

    def greet_sections(k):
        greet((after, k * 2 + core, tensor))
        greet((before, k * 2 + core, tensor))

    loop(1, nd, greet_dp)
    for j in range(1, nt):
        greet((section, dp, tup(j)))
    loop(0, nz, greet_sections)

    src_a[0] = stash_ref[0]
    src_a[1] = grad_ref[...]
    src_b[0] = section_ref[...]
    src_b[1] = stash_ref[1]
    all_a[core, z] = src_a[...]
    all_b[core, z] = src_b[...]
    recv_buf[dp] = jnp.zeros(recv_buf.shape[1:], BF16)

    pl.semaphore_wait(barrier, (nd - 1) + (nt - 1) + 2 * nz)

    def gather_copy(g, src, dst, j, target):
        return remote(src, dst.at[core, z], gather_send.at[g, j], gather_recv.at[g, j], target)

    def gather_start(g, src, dst):
        def send(k):
            j = far_first(k)
            gather_copy(g, src, dst, j, (section, zup(j) * 2 + core, tensor)).start()
        loop(0, nz - 1, send)
        gather_copy(g, src, dst, nz, partner).start()

    def gather_next_start(g, src, dst, target_section):
        def send(k):
            j = far_first(k)
            gather_copy(g, src, dst, j, (target_section, zup(j) * 2 + core, tensor)).start()
        loop(0, nz, send)

    def relay_copy(g, dst, j):
        slot = dst.at[core, zdown(j)]
        return remote(slot, slot, gather_send.at[g, nz + j], gather_recv.at[g, nz + j], partner)

    def relay(g, dst, count):
        def forward(k):
            j = far_first(k)
            slot = dst.at[core, zdown(j)]
            remote(slot, slot, gather_send.at[g, j], gather_recv.at[g, j], partner).wait_recv()
            relay_copy(g, dst, j).start()
        loop(0, count, forward)

    def gather_wait(g, dst):
        def arrive(j):
            slot = dst.at[1 - core, zdown(j)]
            remote(slot, slot, gather_send.at[g, nz + j], gather_recv.at[g, nz + j], partner).wait_recv()
        loop(0, nz, arrive)

    def sum_copy(g, sent, got, j):
        return remote(
            sent.at[pl.ds(pl.multiple_of(tup(j) * part, part), part)], got.at[j],
            tensor_send.at[g, j], tensor_recv.at[g, j], (section, dp, tup(j)),
        )

    def sum_start(g, sent, got):
        for j in range(1, nt):
            sum_copy(g, sent, got, j).start()

    mine = pl.ds(pl.multiple_of(tensor * part, part), part)

    def sum_end(g, sent, got):
        total = sent[mine].astype(F32)
        for j in range(1, nt):
            sum_copy(g, sent, got, j).wait_recv()
            total = total + got[j].astype(F32)
        return total

    def share_copy(g, mix, j):
        return remote(
            mix.at[mine], mix.at[mine], tensor_send.at[g, j], tensor_recv.at[g, j], (section, dp, tup(j))
        )

    def share_start(g, mix):
        for j in range(1, nt):
            share_copy(g, mix, j).start()

    def share_wait(g, mix):
        for j in range(1, nt):
            share_copy(g, mix, j).wait_recv()

    def reduce_start(g, value, keep, half, other):
        keep[...] = value.reshape(2, rows // 2, width)
        half[...] = keep[1 - core].astype(BF16)
        remote(half, other, reduce_send.at[g, 0], reduce_recv.at[g, 0], partner).start()

    def chip_copy(g, chip, got, j):
        return remote(
            chip.at[zup(j)], got.at[z], reduce_send.at[g, j], reduce_recv.at[g, j],
            (section, zup(j) * 2 + core, tensor),
        )

    def reduce_middle(g, keep, half, other, chip, got):
        remote(half, other, reduce_send.at[g, 0], reduce_recv.at[g, 0], partner).wait_recv()
        total = keep[core] + other[...].astype(F32)
        chip[...] = total.reshape(nz, local, width).astype(BF16)
        got[z] = chip[z]

        def send(k):
            chip_copy(g, chip, got, far_first(k)).start()
        loop(0, nz - 1, send)

    def reduce_end(g, chip, got):
        def arrive(j):
            chip_copy(g, chip, got, j).wait_recv()
        loop(1, nz, arrive)
        return jnp.sum(got[...].astype(F32), axis=0)

    def flat_rows(ref):
        return ref[...].astype(F32).reshape(rows, width)

    gain = gain_ref[...].astype(F32)

    def scales_of(lane_squares):
        return lax.rsqrt(jnp.sum(lane_squares, axis=1, keepdims=True) / dw + EPSILON)

    def up_product(widened):
        normed = (widened * gain).astype(BF16)
        product = jnp.dot(normed, up_ref[...], preferred_element_type=F32)
        return normed, product.astype(BF16), lane_blocks_sum(widened * widened).astype(BF16)

    def to_table(table, first, turn, value):
        for b in range(value.shape[1] // BLK):
            table[first + b, turn * rows : (turn + 1) * rows, :] = value[:, b * BLK : (b + 1) * BLK]

    hidden_blocks = hidden // BLK
    channel_blocks = width // BLK
    F0, A_, B_, D1 = 0, 0, 1, 2

    gather_start(0, src_a, all_a)
    gather_start(1, src_b, all_b)

    relay(0, all_a, nz - 1)
    weights_up.wait()
    gather_wait(0, all_a)
    x0 = all_a[:, :, 0].astype(F32).reshape(rows, width)
    normed0, product0, squares0 = up_product(x0)
    sent_p0[:, :hidden] = product0
    sent_p0[:, hidden:] = squares0
    sum_start(0, sent_p0, got_p0)
    weights_down.wait()
    dy0 = all_a[:, :, 1].astype(F32).reshape(rows, width).astype(BF16)
    sent_a0[...] = times_transposed(dy0, down_ref[...]).astype(BF16)
    sum_start(1, sent_a0, got_a0)
    to_table(left_table, 0, 0, normed0)
    to_table(right_table, hidden_blocks, 0, dy0)

    relay(1, all_b, nz - 1)
    gather_wait(1, all_b)
    f0 = all_b[:, :, 0].astype(F32).reshape(rows, width)
    _, product_f0, squares_f0 = up_product(f0)
    sent_f0[:, :hidden] = product_f0
    sent_f0[:, hidden:] = squares_f0
    sum_start(2, sent_f0, got_f0)
    x1 = all_b[:, :, 1].astype(F32).reshape(rows, width)
    normed1, product1, squares1 = up_product(x1)
    sent_p1[:, :hidden] = product1
    sent_p1[:, hidden:] = squares1
    to_table(left_table, 0, 1, normed1)

    def backward_middle(total_p, total_a, mix):
        product, scales = total_p
        inner = product * scales
        gate = jax.nn.sigmoid(inner)
        hidden_grad = total_a * gate * (1.0 + inner * (1.0 - gate))
        mix[mine, :hidden] = (hidden_grad * scales).astype(BF16)
        per_lane = lane_blocks_sum(hidden_grad * product)
        mix[mine, hidden:] = (per_lane * (scales * scales * scales / dw)).astype(BF16)

    def activated_of(product, scales):
        inner = product * scales
        return (inner * jax.nn.sigmoid(inner)).astype(BF16)

    def product_end(g, sent, got):
        total = sum_end(g, sent, got)
        return total[:, :hidden], scales_of(total[:, hidden:])

    total_p0 = product_end(0, sent_p0, got_p0)
    total_a0 = sum_end(1, sent_a0, got_a0)
    backward_middle(total_p0, total_a0, mix_s0)
    share_start(6, mix_s0)
    sum_start(3, sent_p1, got_p1)

    total_f0 = product_end(2, sent_f0, got_f0)
    mix_f0[mine] = activated_of(*total_f0)
    share_start(7, mix_f0)
    mix_h0[mine] = activated_of(*total_p0)
    share_start(8, mix_h0)

    def normed_grad(mix, widened):
        part_sum = times_transposed(mix[:, :hidden], up_ref[...])
        coefficient = jnp.sum(mix[:, hidden:].astype(F32), axis=1, keepdims=True)
        return part_sum * gain - coefficient * widened

    share_wait(6, mix_s0)
    reduce_start(0, normed_grad(mix_s0, all_a[:, :, 0].astype(F32).reshape(rows, width)), keep_b0, half_b0, other_b0)
    to_table(right_table, 0, 0, mix_s0[:, :hidden])

    share_wait(7, mix_f0)
    reduce_start(1, jnp.dot(mix_f0[...], down_ref[...], preferred_element_type=F32), keep_f0, half_f0, other_f0)
    reduce_middle(0, keep_b0, half_b0, other_b0, chip_b0, rows_b0)
    reduce_middle(1, keep_f0, half_f0, other_f0, chip_f0, rows_f0)

    total_p1, scales1 = product_end(3, sent_p1, got_p1)
    held_p1[...] = total_p1
    held_scale1[...] = jnp.broadcast_to(scales1, held_scale1.shape)
    mix_h1[mine] = activated_of(total_p1, scales1)
    share_start(9, mix_h1)

    row_ids = dp * local + lax.broadcasted_iota(jnp.int32, (local, width), 0)
    masked = jnp.where(row_ids < live_ref[0], arriving_ref[...].astype(F32), 0.0)
    input_grad0 = (src_a[1].astype(F32) + reduce_end(0, chip_b0, rows_b0))
    grads_ref[0] = input_grad0.astype(BF16)
    src_d[...] = jnp.where(section == 0, masked, input_grad0).astype(BF16)
    gather_next_start(2, src_d, all_d, before)

    output0 = src_b[0].astype(F32) + reduce_end(1, chip_f0, rows_f0)
    outputs_ref[0] = output0.astype(BF16)
    src_f[...] = jnp.where(section == ns - 1, entering_ref[...].astype(F32), output0).astype(BF16)
    gather_next_start(3, src_f, all_f, after)

    share_wait(8, mix_h0)
    to_table(left_table, channel_blocks, 0, mix_h0[...])
    share_wait(9, mix_h1)
    to_table(left_table, channel_blocks, 1, mix_h1[...])

    capacity = owner_ref.shape[1]
    up_count = hidden_blocks * channel_blocks
    left_index, right_index = [], []
    for k in range(capacity):
        number = blocks_ref[dp, k]
        down_number = jnp.maximum(number - up_count, 0)
        is_up = number < up_count
        left_index.append(
            jnp.where(is_up, number // hidden_blocks, channel_blocks + down_number // channel_blocks)
        )
        right_index.append(
            jnp.where(is_up, number % hidden_blocks, hidden_blocks + down_number % channel_blocks)
        )
    my_count = count_ref[dp]
    my_owners = [owner_ref[dp, k] for k in range(capacity)]
    picks = []
    for o in range(nd):
        pick = jnp.int32(0)
        for k in range(capacity):
            pick = jnp.where((my_owners[k] == o) & (k < my_count), k, pick)
        picks.append(pick)
    taken = jnp.int32(0)
    sources = [jnp.int32(0) for _ in range(capacity)]
    for h in range(nd):
        sends = jnp.int32(0)
        for k in range(capacity):
            sends = jnp.where((owner_ref[h, k] == dp) & (k < count_ref[h]), 1, sends)
        for i in range(capacity):
            sources[i] = jnp.where((sends == 1) & (taken == i), h, sources[i])
        taken = taken + sends

    relay(2, all_d, nz)
    gather_wait(2, all_d)
    dy1 = flat_rows(all_d).astype(BF16)
    sent_a1[...] = times_transposed(dy1, down_ref[...]).astype(BF16)
    sum_start(4, sent_a1, got_a1)
    to_table(right_table, hidden_blocks, 1, dy1)

    relay(3, all_f, nz)
    gather_wait(3, all_f)
    f1 = flat_rows(all_f)
    _, product_f1, squares_f1 = up_product(f1)
    sent_f1[:, :hidden] = product_f1
    sent_f1[:, hidden:] = squares_f1
    sum_start(5, sent_f1, got_f1)

    total_a1 = sum_end(4, sent_a1, got_a1)
    backward_middle((held_p1[...], held_scale1[:, :1]), total_a1, mix_s1)
    share_start(10, mix_s1)

    total_f1 = product_end(5, sent_f1, got_f1)
    mix_f1[mine] = activated_of(*total_f1)
    share_start(11, mix_f1)

    share_wait(10, mix_s1)
    to_table(right_table, 0, 1, mix_s1[:, :hidden])
    for k in range(capacity):
        block = lax.dot_general(
            left_table[left_index[k]], right_table[right_index[k]],
            (((0,), (0,)), ((), ())), preferred_element_type=F32,
        )
        block_buf[k] = block.astype(BF16)
    for o in range(nd):
        send_buf[o] = block_buf[picks[o]]

    def block_copy(j):
        owner = lax.rem(dp + j, nd)
        return remote(
            send_buf.at[owner], recv_buf.at[dp], block_send.at[j], block_recv.at[j],
            (section, owner, tensor),
        )

    def send_block(k):
        block_copy(nz + (1 - 2 * (k % 2)) * ((k + 1) // 2)).start()
    loop(0, nd - 1, send_block)

    reduce_start(2, normed_grad(mix_s1, all_b[:, :, 1].astype(F32).reshape(rows, width)), keep_b1, half_b1, other_b1)
    share_wait(11, mix_f1)
    reduce_start(3, jnp.dot(mix_f1[...], down_ref[...], preferred_element_type=F32), keep_f1, half_f1, other_f1)
    reduce_middle(2, keep_b1, half_b1, other_b1, chip_b1, rows_b1)
    reduce_middle(3, keep_f1, half_f1, other_f1, chip_f1, rows_f1)
    grads_ref[1] = (all_d[core, z].astype(F32) + reduce_end(2, chip_b1, rows_b1)).astype(BF16)
    outputs_ref[1] = (all_f[core, z].astype(F32) + reduce_end(3, chip_f1, rows_f1)).astype(BF16)

    def got_block(j):
        source = lax.rem(dp + nd - j, nd)
        remote(
            send_buf.at[source], recv_buf.at[source], block_send.at[j], block_recv.at[j],
            (section, source, tensor),
        ).wait_recv()
    loop(1, nd, got_block)
    for i in range(capacity):
        owned_ref[i] = jnp.where(i < taken, recv_buf[sources[i]].astype(F32), 0.0)
        filled_ref[i] = jnp.where(i < taken, jnp.ones((1, LANES), F32), 0.0)

    for g, src, dst in ((0, src_a, all_a), (1, src_b, all_b)):
        def left_gather(j, g=g, src=src, dst=dst):
            gather_copy(g, src, dst, j, partner).wait_send()
            relay_copy(g, dst, j).wait_send()
        loop(1, nz, left_gather)
        gather_copy(g, src, dst, nz, partner).wait_send()
    for g, src, dst in ((2, src_d, all_d), (3, src_f, all_f)):
        def left_next(j, g=g, src=src, dst=dst):
            gather_copy(g, src, dst, j, partner).wait_send()
            relay_copy(g, dst, j).wait_send()
        loop(0, nz, left_next)
    for g, sent, got in (
        (0, sent_p0, got_p0), (1, sent_a0, got_a0), (2, sent_f0, got_f0),
        (3, sent_p1, got_p1), (4, sent_a1, got_a1), (5, sent_f1, got_f1),
    ):
        for j in range(1, nt):
            sum_copy(g, sent, got, j).wait_send()
    for g, mix in ((6, mix_s0), (7, mix_f0), (8, mix_h0), (9, mix_h1), (10, mix_s1), (11, mix_f1)):
        for j in range(1, nt):
            share_copy(g, mix, j).wait_send()
    for g, half, other, chip, got in (
        (0, half_b0, other_b0, chip_b0, rows_b0), (1, half_f0, other_f0, chip_f0, rows_f0),
        (2, half_b1, other_b1, chip_b1, rows_b1), (3, half_f1, other_f1, chip_f1, rows_f1),
    ):
        remote(half, other, reduce_send.at[g, 0], reduce_recv.at[g, 0], partner).wait_send()
        def left_reduce(j, g=g, chip=chip, got=got):
            chip_copy(g, chip, got, j).wait_send()
        loop(1, nz, left_reduce)

    def left_block(j):
        block_copy(j).wait_send()
    loop(1, nd, left_block)


def body(
    sizes,
    section_inputs, entering, grad_outputs, arriving, live_rows, stashed_inputs, norm_gain,
    up_weight, down_weight, held_blocks, held_count, held_owner, first_moment, second_moment,
):
    ns, nz, nt = sizes
    nd = 2 * nz
    local, width = section_inputs.shape[1:]
    hidden = up_weight.shape[2]
    rows = local * nd
    part = rows // nt
    capacity = held_owner.shape[3]
    turns = stashed_inputs.shape[1]
    blocks = hidden // BLK + width // BLK
    smem = pl.BlockSpec(memory_space=pltpu.SMEM)
    vmem = pl.BlockSpec(memory_space=pltpu.VMEM)
    anywhere = pl.BlockSpec(memory_space=pl.ANY)
    wide = hidden + LANES

    def several(count, shape, dtype):
        return [pltpu.VMEM(shape, dtype) for _ in range(count)]

    scratch = [
        pltpu.VMEM((width, hidden), BF16), pltpu.VMEM((hidden, width), BF16),
        *several(2, (2, local, width), BF16),
        *several(2, (2, nz, 2, local, width), BF16),
        *several(2, (local, width), BF16),
        *several(2, (2, nz, local, width), BF16),
        *[pltpu.VMEM((rows, w), BF16) for w in (wide, hidden, wide, wide, hidden, wide)],
        *[pltpu.VMEM((nt, part, w), BF16) for w in (wide, hidden, wide, wide, hidden, wide)],
        *[pltpu.VMEM((rows, w), BF16) for w in (wide, hidden, hidden, hidden, wide, hidden)],
        *several(4, (2, rows // 2, width), F32),
        *several(4, (rows // 2, width), BF16),
        *several(4, (rows // 2, width), BF16),
        *several(4, (nz, local, width), BF16),
        *several(4, (nz, local, width), BF16),
        *several(2, (blocks, turns * rows, BLK), BF16),
        pltpu.VMEM((capacity, BLK, BLK), BF16),
        *several(2, (nd, BLK, BLK), BF16),
        pltpu.VMEM((part, hidden), F32), pltpu.VMEM((part, LANES), F32),
        pltpu.SemaphoreType.DMA((2,)),
        pltpu.SemaphoreType.DMA((4, 2 * nz)), pltpu.SemaphoreType.DMA((4, 2 * nz)),
        pltpu.SemaphoreType.DMA((12, nt)), pltpu.SemaphoreType.DMA((12, nt)),
        pltpu.SemaphoreType.DMA((4, nz)), pltpu.SemaphoreType.DMA((4, nz)),
        pltpu.SemaphoreType.DMA((nd,)), pltpu.SemaphoreType.DMA((nd,)),
    ]
    outputs, grads, owned, filled = pl.pallas_call(
        functools.partial(kernel, sizes),
        out_shape=(
            jax.ShapeDtypeStruct((turns, local, width), BF16),
            jax.ShapeDtypeStruct((turns, local, width), BF16),
            jax.ShapeDtypeStruct((capacity, BLK, BLK), F32),
            jax.ShapeDtypeStruct((capacity, 1, LANES), F32),
        ),
        in_specs=[smem] * 4 + [vmem] * 6 + [anywhere] * 2,
        out_specs=[vmem] * 4,
        scratch_shapes=scratch,
        compiler_params=pltpu.CompilerParams(
            collective_id=0, has_side_effects=True, vmem_limit_bytes=56 * 1024 * 1024
        ),
        name="relay",
    )(
        live_rows, held_blocks[0, 0], held_count[0, 0], held_owner[0, 0],
        section_inputs[0], entering[0], grad_outputs[0], arriving[0], stashed_inputs[0], norm_gain,
        up_weight[0], down_weight[0],
    )
    is_filled = filled[:, :, :1] > 0.5
    first_new = 0.9 * first_moment[0, 0, 0] + 0.1 * owned
    second_new = 0.999 * second_moment[0, 0, 0] + 0.001 * owned * owned
    direction = first_new / (jnp.sqrt(second_new) + 1e-08)
    first_out = jnp.where(is_filled, first_new, 0.0)
    second_out = jnp.where(is_filled, second_new, 0.0)
    direction_out = jnp.where(is_filled, direction, 0.0)
    return (
        outputs[None], grads[None],
        first_out[None, None, None], second_out[None, None, None], direction_out[None, None, None],
    )


def solution(mesh):
    sizes = (mesh.shape["section"], mesh.shape["dp"] // 2, mesh.shape["tensor"])
    return jax.shard_map(
        functools.partial(body, sizes),
        mesh=mesh,
        in_specs=(
            P("section", "dp", "tensor"),
            P(None, "dp", "tensor"),
            P("section", "dp", "tensor"),
            P(None, "dp", "tensor"),
            P(),
            P("section", None, "dp", "tensor"),
            P("section", "tensor"),
            P("section", "tensor", "dp"),
            P("section", "dp", "tensor"),
            P("section", "tensor", None, None),
            P("section", "tensor", None),
            P("section", "tensor", None, None),
            P("section", "tensor", "dp", None, None, None),
            P("section", "tensor", "dp", None, None, None),
        ),
        out_specs=(
            P("section", None, "dp", "tensor"),
            P("section", None, "dp", "tensor"),
            P("section", "tensor", "dp", None, None, None),
            P("section", "tensor", "dp", None, None, None),
            P("section", "tensor", "dp", None, None, None),
        ),
        check_vma=False,
    )
```

time: 779 us -> 97.5 us (0.13)
  waiting for transfers between devices: 507 us -> 0 us
  blocking collectives: 185 us -> 0 us
  Pallas kernels: 0 us -> 87.8 us
  other arithmetic: 22 us -> 3.04 us
  matrix products: 15.5 us -> 0 us
  between operations: 16 us -> 1.32 us
  starting transfers between devices: 14.6 us -> 0 us
  local copies, waits for them, and re-layouts: 18.4 us -> 3.95 us
    unnamed x12 -> x0, waiting for transfers between devices: 359 us -> none
    psum x4 -> x0, waiting for transfers between devices: 147 us -> none  [the longest x2 93.6 us: body(): lax.psum(forward_product.astype(jnp.bfloat16), 'tensor').astype(jnp.float32)]
    all_gather x6 -> x0, blocking collectives: 109 us -> none  [the longest x2 41.1 us: body(): rows_all = lax.all_gather(rows_local, 'dp', axis=0, tiled=True)]
    pallas_call x0 -> x1, Pallas kernels: none -> 87.8 us  [body(): pl.pallas_call(functools.partial(kernel, sizes), out_shape=(jax.ShapeDtyp...]
    unnamed x2 -> x0, blocking collectives: 51.2 us -> none
    psum x3 -> x0, blocking collectives: 25.5 us -> none  [the longest x2 16.6 us: body(): lax.psum(forward_squares.astype(jnp.bfloat16), 'tensor').astype(jnp.float32)]
    dot_general x12 -> x0, matrix products: 15.5 us -> none  [the longest x4 4.89 us: normed_product(): product = jnp.dot(normed, up_matrix, preferred_element_type=jnp.float32)]
    all_to_all x1 -> x0, starting transfers between devices: 9.7 us -> none  [body(): lax.all_to_all(outgoing, 'dp', split_axis=0, concat_axis=0, tiled=True)]
  transfers between devices with their start and end apart: 11 -> 0, of which waited for: 8 -> 0; matrix products, arithmetic and copies ran while one was open for 4% -> 0% of each run, Pallas kernels for 0% -> 0%
where the time goes in v1:
time: 97.5 us; the launch traced here: 96.1 us
  Pallas kernels  87.8 us (90%)
  local copies, waits for them, and re-layouts  3.95 us (4%)
  other arithmetic  3.04 us (3%)
  between operations  1.32 us (1%)
    pallas_call x1, Pallas kernels, body(): pl.pallas_call(functools.partial(kernel, sizes), out_shape=(jax.ShapeDtyp...  87.8 us
    broadcast_in_dim x1, other arithmetic, body(): direction_out[None, None, None]  2.16 us

profile of v1, /device:TPU:1, one launch (start us, length us, event | category | flops | bytes accessed | tf_op | source)
XLA Modules:
  0.0 96.1 jit_solution(12755349795691002943)
XLA Ops:
  1.3 1.4 %copy.23 = s32[1,1,16,6]{3,2,1,0:T(8,128)} copy(s32[1,1,16,6]{2,1,3,0:T(1,128)} %param.23) | data formatting | bytes 768 | tf_op jit(solution)/shard_map/squeeze | solution.py:527
  2.6 1.4 %copy.24 = s32[1,1,16,6]{3,2,1,0:T(8,128)} copy(s32[1,1,16,6]{2,1,3,0:T(1,128)} %param.25) | data formatting | bytes 768 | tf_op jit(solution)/shard_map/squeeze | solution.py:527
  4.0 0.0 copy-start
  4.0 0.0 copy-start.1
  4.0 87.8 %relay.1 = (bf16[2,8,640]{2,1,0:T(8,128)(2,1)}, bf16[2,8,640]{2,1,0:T(8,128)(2,1)}, f32[6,128,128]{2,1,0:T(8,128)}, f32[6,1,128]{2,1,0:T(1,128)}) custom-call(s32[1]{0:T(128)S(6)} %copy.27.live_ref, s32[16,6]{1,0:T(8,128)} %bitcast.32, s32[16]{0:T(128)} %bitcast.41, s32[16,6]{1,0:T(8,128)} %bitcast.33, bf16[8,640]{1,0:T(8,128)(2,1)} %bitcast.37, ...), custom_call_target="tpu_custom_call" | custom-call | tf_op jit(solution)/shard_map/relay/pallas_call | solution.py:511
  91.8 0.9 compare_reduce_fusion
  92.7 0.0 copy-done
  92.7 0.0 copy-done.1
  92.7 0.0 copy-start.3
  92.7 0.0 copy-start.2
  92.7 2.2 %select_bitcast_fusion = (f32[1,1,1,6,128,128]{5,4,3,2,1,0:T(8,128)}, f32[1,1,1,6,128,128]{5,4,3,2,1,0:T(8,128)}, f32[1,1,1,6,128,128]{5,4,3,2,1,0:T(8,128)}) fusion(pred[6]{0:T(512)(128)(4,1)S(1)} %compare_reduce_fusion, f32[6,128,128]{2,1,0:T(8,128)} %get-tuple-element.12, f32[1,1,1,6,128,128]{5,4,3,2,1,0:T(8,128)S(1)} %copy-done, ...), kind=kLoop, calls=%fused_computation.3 | loop fusion | flops 1179648 | bytes 2359302 | tf_op jit(solution)/shard_map/broadcast_in_dim | solution.py:540
  94.9 0.0 copy-done.3
  94.9 0.6 copy.28
  95.5 0.0 copy-done.2
  95.5 0.6 copy.29
Async XLA Ops:
  4.0 88.7 %copy-start = (f32[1,1,1,6,128,128]{5,4,3,2,1,0:T(8,128)S(1)}, f32[1,1,1,6,128,128]{5,4,3,2,1,0:T(8,128)}, u32[]{:S(2)}) copy-start(f32[1,1,1,6,128,128]{5,4,3,2,1,0:T(8,128)} %param.26) | copy-start | bytes 1179652
  4.0 88.7 %copy-start.1 = (f32[1,1,1,6,128,128]{5,4,3,2,1,0:T(8,128)S(1)}, f32[1,1,1,6,128,128]{5,4,3,2,1,0:T(8,128)}, u32[]{:S(2)}) copy-start(f32[1,1,1,6,128,128]{5,4,3,2,1,0:T(8,128)} %param.27) | copy-start | bytes 1179652
  92.7 2.2 %copy-start.3 = (bf16[2,8,640]{2,1,0:T(8,128)(2,1)S(1)}, bf16[2,8,640]{2,1,0:T(8,128)(2,1)}, u32[]{:S(2)}) copy-start(bf16[2,8,640]{2,1,0:T(8,128)(2,1)} %get-tuple-element.9) | copy-start | bytes 61444
  92.7 2.8 %copy-start.2 = (bf16[2,8,640]{2,1,0:T(8,128)(2,1)S(1)}, bf16[2,8,640]{2,1,0:T(8,128)(2,1)}, u32[]{:S(2)}) copy-start(bf16[2,8,640]{2,1,0:T(8,128)(2,1)} %get-tuple-element.10) | copy-start | bytes 61444

commit v2 on v1

--- a/solution.py
+++ b/solution.py
@@ -29,22 +29,24 @@
 def kernel(
     sizes,
     live_ref, blocks_ref, count_ref, owner_ref,
-    section_ref, entering_ref, grad_ref, arriving_ref, stash_ref, gain_ref,
+    section_hbm, entering_hbm, grad_hbm, arriving_hbm, stash_hbm, gain_hbm,
     up_hbm, down_hbm,
     outputs_ref, grads_ref, owned_ref, filled_ref,
     up_ref, down_ref,
+    entering_ref, arriving_ref, gain_ref,
     src_a, src_b, all_a, all_b, src_f, src_d, all_f, all_d,
     sent_p0, sent_a0, sent_f0, sent_p1, sent_a1, sent_f1,
     got_p0, got_a0, got_f0, got_p1, got_a1, got_f1,
     mix_s0, mix_h0, mix_f0, mix_h1, mix_s1, mix_f1,
-    keep_b0, keep_f0, keep_b1, keep_f1,
-    half_b0, half_f0, half_b1, half_f1,
-    other_b0, other_f0, other_b1, other_f1,
-    chip_b0, chip_f0, chip_b1, chip_f1,
-    rows_b0, rows_f0, rows_b1, rows_f1,
+    keep_f0, keep_b1, keep_f1,
+    half_f0, half_b1, half_f1,
+    other_f0, other_b1, other_f1,
+    chip_f0, chip_b1, chip_f1,
+    rows_f0, rows_b1, rows_f1,
+    parts_b0, rows_b0,
     left_table, right_table, block_buf, send_buf, recv_buf,
     held_p1, held_scale1,
-    weight_sem,
+    weight_sem, input_sem,
     gather_send, gather_recv,
     tensor_send, tensor_recv,
     reduce_send, reduce_recv,
@@ -52,7 +54,7 @@
 ):
     ns, nz, nt = sizes
     nd = 2 * nz
-    local, width = section_ref.shape
+    local, width = entering_ref.shape
     hidden = up_ref.shape[1]
     rows = local * nd
     part = rows // nt
@@ -66,6 +68,9 @@
     after = lax.rem(section + 1, ns)
     before = lax.rem(section + ns - 1, ns)
 
+    leaving = []
+    coming = {}
+
     def remote(src, dst, send_sem, recv_sem, device):
         return pltpu.make_async_remote_copy(
             src_ref=src, dst_ref=dst, send_sem=send_sem, recv_sem=recv_sem,
@@ -92,8 +97,6 @@
 
     weights_up = pltpu.make_async_copy(up_hbm, up_ref, weight_sem.at[0])
     weights_down = pltpu.make_async_copy(down_hbm, down_ref, weight_sem.at[1])
-    weights_up.start()
-    weights_down.start()
 
     barrier = pltpu.get_barrier_semaphore()
 
@@ -112,12 +115,22 @@
         greet((section, dp, tup(j)))
     loop(0, nz, greet_sections)
 
-    src_a[0] = stash_ref[0]
-    src_a[1] = grad_ref[...]
-    src_b[0] = section_ref[...]
-    src_b[1] = stash_ref[1]
-    all_a[core, z] = src_a[...]
-    all_b[core, z] = src_b[...]
+    inputs = [
+        pltpu.make_async_copy(src, dst, input_sem.at[i])
+        for i, (src, dst) in enumerate((
+            (stash_hbm.at[0], src_a.at[0]), (grad_hbm, src_a.at[1]),
+            (section_hbm, src_b.at[0]), (stash_hbm.at[1], src_b.at[1]),
+            (stash_hbm.at[0], all_a.at[core, z, 0]), (grad_hbm, all_a.at[core, z, 1]),
+            (section_hbm, all_b.at[core, z, 0]), (stash_hbm.at[1], all_b.at[core, z, 1]),
+            (entering_hbm, entering_ref), (arriving_hbm, arriving_ref), (gain_hbm, gain_ref),
+        ))
+    ]
+    for copy in inputs:
+        copy.start()
+    weights_up.start()
+    weights_down.start()
+    for copy in inputs:
+        copy.wait()
     recv_buf[dp] = jnp.zeros(recv_buf.shape[1:], BF16)
 
     pl.semaphore_wait(barrier, (nd - 1) + (nt - 1) + 2 * nz)
@@ -132,11 +145,21 @@
         loop(0, nz - 1, send)
         gather_copy(g, src, dst, nz, partner).start()
 
+        def left(j):
+            gather_copy(g, src, dst, j, partner).wait_send()
+        leaving.append(lambda: loop(1, nz + 1, left))
+        coming["gather", g] = lambda: (relay(g, dst, nz - 1), gather_wait(g, dst))
+
     def gather_next_start(g, src, dst, target_section):
         def send(k):
             j = far_first(k)
             gather_copy(g, src, dst, j, (target_section, zup(j) * 2 + core, tensor)).start()
         loop(0, nz, send)
+
+        def left(j):
+            gather_copy(g, src, dst, j, partner).wait_send()
+        leaving.append(lambda: loop(0, nz, left))
+        coming["gather", g] = lambda: (relay(g, dst, nz), gather_wait(g, dst))
 
     def relay_copy(g, dst, j):
         slot = dst.at[core, zdown(j)]
@@ -150,12 +173,48 @@
             relay_copy(g, dst, j).start()
         loop(0, count, forward)
 
+        def left(j):
+            relay_copy(g, dst, j).wait_send()
+        leaving.append(lambda: loop(nz - count, nz, left))
+
     def gather_wait(g, dst):
+        coming.pop(("gather", g))
+
         def arrive(j):
             slot = dst.at[1 - core, zdown(j)]
             remote(slot, slot, gather_send.at[g, nz + j], gather_recv.at[g, nz + j], partner).wait_recv()
         loop(0, nz, arrive)
 
+    def both_copy(g, src, dst, j, other_core, target_section):
+        return remote(
+            src, dst.at[core, z],
+            gather_send.at[g, 2 * j + other_core], gather_recv.at[g, 2 * j + other_core],
+            (target_section, zup(j) * 2 + lax.rem(core + other_core, 2), tensor),
+        )
+
+    def both_start(g, src, dst, target_section):
+        def send(k):
+            j = far_first(k)
+            both_copy(g, src, dst, j, 0, target_section).start()
+            both_copy(g, src, dst, j, 1, target_section).start()
+        loop(0, nz, send)
+
+        def left(j):
+            both_copy(g, src, dst, j, 0, target_section).wait_send()
+            both_copy(g, src, dst, j, 1, target_section).wait_send()
+        leaving.append(lambda: loop(0, nz, left))
+        coming["both", g] = lambda: both_wait(g, dst)
+
+    def both_wait(g, dst):
+        coming.pop(("both", g))
+
+        def arrive(j):
+            for other_core in range(2):
+                slot = dst.at[lax.rem(core + other_core, 2), zdown(j)]
+                sem = 2 * j + other_core
+                remote(slot, slot, gather_send.at[g, sem], gather_recv.at[g, sem], partner).wait_recv()
+        loop(0, nz, arrive)
+
     def sum_copy(g, sent, got, j):
         return remote(
             sent.at[pl.ds(pl.multiple_of(tup(j) * part, part), part)], got.at[j],
@@ -165,10 +224,13 @@
     def sum_start(g, sent, got):
         for j in range(1, nt):
             sum_copy(g, sent, got, j).start()
+            leaving.append(lambda j=j: sum_copy(g, sent, got, j).wait_send())
+        coming["sum", g] = lambda: sum_end(g, sent, got)
 
     mine = pl.ds(pl.multiple_of(tensor * part, part), part)
 
     def sum_end(g, sent, got):
+        coming.pop(("sum", g))
         total = sent[mine].astype(F32)
         for j in range(1, nt):
             sum_copy(g, sent, got, j).wait_recv()
@@ -183,15 +245,21 @@
     def share_start(g, mix):
         for j in range(1, nt):
             share_copy(g, mix, j).start()
+            leaving.append(lambda j=j: share_copy(g, mix, j).wait_send())
+        coming["share", g] = lambda: share_wait(g, mix)
 
     def share_wait(g, mix):
+        coming.pop(("share", g))
         for j in range(1, nt):
             share_copy(g, mix, j).wait_recv()
 
     def reduce_start(g, value, keep, half, other):
         keep[...] = value.reshape(2, rows // 2, width)
         half[...] = keep[1 - core].astype(BF16)
-        remote(half, other, reduce_send.at[g, 0], reduce_recv.at[g, 0], partner).start()
+        swap = remote(half, other, reduce_send.at[g, 0], reduce_recv.at[g, 0], partner)
+        swap.start()
+        leaving.append(swap.wait_send)
+        coming["swap", g] = swap.wait_recv
 
     def chip_copy(g, chip, got, j):
         return remote(
@@ -200,7 +268,7 @@
         )
 
     def reduce_middle(g, keep, half, other, chip, got):
-        remote(half, other, reduce_send.at[g, 0], reduce_recv.at[g, 0], partner).wait_recv()
+        coming.pop(("swap", g))()
         total = keep[core] + other[...].astype(F32)
         chip[...] = total.reshape(nz, local, width).astype(BF16)
         got[z] = chip[z]
@@ -209,12 +277,60 @@
             chip_copy(g, chip, got, far_first(k)).start()
         loop(0, nz - 1, send)
 
+        def left(j):
+            chip_copy(g, chip, got, j).wait_send()
+        leaving.append(lambda: loop(1, nz, left))
+        coming["reduce", g] = lambda: reduce_end(g, chip, got)
+
     def reduce_end(g, chip, got):
+        coming.pop(("reduce", g))
+
         def arrive(j):
             chip_copy(g, chip, got, j).wait_recv()
         loop(1, nz, arrive)
         return jnp.sum(got[...].astype(F32), axis=0)
 
+    def scatter_copy(g, parts, got, j, other_core):
+        target = lax.rem(core + other_core, 2)
+        return remote(
+            parts.at[target, zup(j)], got.at[dp],
+            reduce_send.at[g, 2 * j + other_core], reduce_recv.at[g, 2 * j + other_core],
+            (section, zup(j) * 2 + target, tensor),
+        )
+
+    def scatter_start(g, value, parts, got):
+        parts[...] = value.reshape(parts.shape).astype(BF16)
+        got[dp] = parts[core, z]
+
+        def send(k):
+            j = far_first(k)
+            scatter_copy(g, parts, got, j, 0).start()
+            scatter_copy(g, parts, got, j, 1).start()
+        loop(0, nz - 1, send)
+        scatter_copy(g, parts, got, 0, 1).start()
+
+        def left(j):
+            scatter_copy(g, parts, got, j, 0).wait_send()
+            scatter_copy(g, parts, got, j, 1).wait_send()
+        leaving.append(lambda: loop(1, nz, left))
+        leaving.append(lambda: scatter_copy(g, parts, got, 0, 1).wait_send())
+        coming["scatter", g] = lambda: scatter_end(g, parts, got)
+
+    def scatter_end(g, parts, got):
+        coming.pop(("scatter", g))
+
+        def arrive(j, other_core):
+            slot = got.at[zdown(j) * 2 + lax.rem(core + other_core, 2)]
+            sem = 2 * j + other_core
+            remote(slot, slot, reduce_send.at[g, sem], reduce_recv.at[g, sem], partner).wait_recv()
+
+        def arrive_both(j):
+            arrive(j, 0)
+            arrive(j, 1)
+        loop(1, nz, arrive_both)
+        arrive(0, 1)
+        return jnp.sum(got[...].astype(F32), axis=0)
+
     def flat_rows(ref):
         return ref[...].astype(F32).reshape(rows, width)
 
@@ -234,38 +350,6 @@
 
     hidden_blocks = hidden // BLK
     channel_blocks = width // BLK
-    F0, A_, B_, D1 = 0, 0, 1, 2
-
-    gather_start(0, src_a, all_a)
-    gather_start(1, src_b, all_b)
-
-    relay(0, all_a, nz - 1)
-    weights_up.wait()
-    gather_wait(0, all_a)
-    x0 = all_a[:, :, 0].astype(F32).reshape(rows, width)
-    normed0, product0, squares0 = up_product(x0)
-    sent_p0[:, :hidden] = product0
-    sent_p0[:, hidden:] = squares0
-    sum_start(0, sent_p0, got_p0)
-    weights_down.wait()
-    dy0 = all_a[:, :, 1].astype(F32).reshape(rows, width).astype(BF16)
-    sent_a0[...] = times_transposed(dy0, down_ref[...]).astype(BF16)
-    sum_start(1, sent_a0, got_a0)
-    to_table(left_table, 0, 0, normed0)
-    to_table(right_table, hidden_blocks, 0, dy0)
-
-    relay(1, all_b, nz - 1)
-    gather_wait(1, all_b)
-    f0 = all_b[:, :, 0].astype(F32).reshape(rows, width)
-    _, product_f0, squares_f0 = up_product(f0)
-    sent_f0[:, :hidden] = product_f0
-    sent_f0[:, hidden:] = squares_f0
-    sum_start(2, sent_f0, got_f0)
-    x1 = all_b[:, :, 1].astype(F32).reshape(rows, width)
-    normed1, product1, squares1 = up_product(x1)
-    sent_p1[:, :hidden] = product1
-    sent_p1[:, hidden:] = squares1
-    to_table(left_table, 0, 1, normed1)
 
     def backward_middle(total_p, total_a, mix):
         product, scales = total_p
@@ -284,31 +368,68 @@
         total = sum_end(g, sent, got)
         return total[:, :hidden], scales_of(total[:, hidden:])
 
+    def normed_grad(mix, widened):
+        part_sum = times_transposed(mix[:, :hidden], up_ref[...])
+        coefficient = jnp.sum(mix[:, hidden:].astype(F32), axis=1, keepdims=True)
+        return part_sum * gain - coefficient * widened
+
+    def stored_product(ref, product, lane_squares):
+        ref[:, :hidden] = product
+        ref[:, hidden:] = lane_squares
+
+    def rows_of(ref, which):
+        return ref[:, :, which].astype(F32).reshape(rows, width)
+
+    gather_start(0, src_a, all_a)
+    gather_start(1, src_b, all_b)
+
+    relay(0, all_a, nz - 1)
+    weights_up.wait()
+    gather_wait(0, all_a)
+    normed0, *made = up_product(rows_of(all_a, 0))
+    stored_product(sent_p0, *made)
+    sum_start(0, sent_p0, got_p0)
+    weights_down.wait()
+    dy0 = rows_of(all_a, 1).astype(BF16)
+    sent_a0[...] = times_transposed(dy0, down_ref[...]).astype(BF16)
+    sum_start(1, sent_a0, got_a0)
+    to_table(left_table, 0, 0, normed0)
+    to_table(right_table, hidden_blocks, 0, dy0)
+
+    relay(1, all_b, nz - 1)
+    gather_wait(1, all_b)
+    normed, product, lane_squares = up_product(jnp.concatenate([rows_of(all_b, 0), rows_of(all_b, 1)]))
+    stored_product(sent_f0, product[:rows], lane_squares[:rows])
+    sum_start(2, sent_f0, got_f0)
+    stored_product(sent_p1, product[rows:], lane_squares[rows:])
+    to_table(left_table, 0, 1, normed[rows:])
+
     total_p0 = product_end(0, sent_p0, got_p0)
     total_a0 = sum_end(1, sent_a0, got_a0)
     backward_middle(total_p0, total_a0, mix_s0)
     share_start(6, mix_s0)
-    sum_start(3, sent_p1, got_p1)
 
     total_f0 = product_end(2, sent_f0, got_f0)
     mix_f0[mine] = activated_of(*total_f0)
     share_start(7, mix_f0)
     mix_h0[mine] = activated_of(*total_p0)
+
+    share_wait(6, mix_s0)
+    scatter_start(0, normed_grad(mix_s0, rows_of(all_a, 0)), parts_b0, rows_b0)
+    sum_start(3, sent_p1, got_p1)
     share_start(8, mix_h0)
-
-    def normed_grad(mix, widened):
-        part_sum = times_transposed(mix[:, :hidden], up_ref[...])
-        coefficient = jnp.sum(mix[:, hidden:].astype(F32), axis=1, keepdims=True)
-        return part_sum * gain - coefficient * widened
-
-    share_wait(6, mix_s0)
-    reduce_start(0, normed_grad(mix_s0, all_a[:, :, 0].astype(F32).reshape(rows, width)), keep_b0, half_b0, other_b0)
     to_table(right_table, 0, 0, mix_s0[:, :hidden])
 
     share_wait(7, mix_f0)
     reduce_start(1, jnp.dot(mix_f0[...], down_ref[...], preferred_element_type=F32), keep_f0, half_f0, other_f0)
-    reduce_middle(0, keep_b0, half_b0, other_b0, chip_b0, rows_b0)
     reduce_middle(1, keep_f0, half_f0, other_f0, chip_f0, rows_f0)
+
+    row_ids = dp * local + lax.broadcasted_iota(jnp.int32, (local, width), 0)
+    masked = jnp.where(row_ids < live_ref[0], arriving_ref[...].astype(F32), 0.0)
+    input_grad0 = src_a[1].astype(F32) + scatter_end(0, parts_b0, rows_b0)
+    src_d[...] = jnp.where(section == 0, masked, input_grad0).astype(BF16)
+    both_start(2, src_d, all_d, before)
+    grads_ref[0] = input_grad0.astype(BF16)
 
     total_p1, scales1 = product_end(3, sent_p1, got_p1)
     held_p1[...] = total_p1
@@ -316,28 +437,19 @@
     mix_h1[mine] = activated_of(total_p1, scales1)
     share_start(9, mix_h1)
 
-    row_ids = dp * local + lax.broadcasted_iota(jnp.int32, (local, width), 0)
-    masked = jnp.where(row_ids < live_ref[0], arriving_ref[...].astype(F32), 0.0)
-    input_grad0 = (src_a[1].astype(F32) + reduce_end(0, chip_b0, rows_b0))
-    grads_ref[0] = input_grad0.astype(BF16)
-    src_d[...] = jnp.where(section == 0, masked, input_grad0).astype(BF16)
-    gather_next_start(2, src_d, all_d, before)
-
     output0 = src_b[0].astype(F32) + reduce_end(1, chip_f0, rows_f0)
-    outputs_ref[0] = output0.astype(BF16)
     src_f[...] = jnp.where(section == ns - 1, entering_ref[...].astype(F32), output0).astype(BF16)
     gather_next_start(3, src_f, all_f, after)
+    outputs_ref[0] = output0.astype(BF16)
 
     share_wait(8, mix_h0)
     to_table(left_table, channel_blocks, 0, mix_h0[...])
-    share_wait(9, mix_h1)
-    to_table(left_table, channel_blocks, 1, mix_h1[...])
-
-    capacity = owner_ref.shape[1]
+
+    capacity = owner_ref.shape[0]
     up_count = hidden_blocks * channel_blocks
     left_index, right_index = [], []
     for k in range(capacity):
-        number = blocks_ref[dp, k]
+        number = blocks_ref[k, 0, dp]
         down_number = jnp.maximum(number - up_count, 0)
         is_up = number < up_count
         left_index.append(
@@ -347,7 +459,7 @@
             jnp.where(is_up, number % hidden_blocks, hidden_blocks + down_number % channel_blocks)
         )
     my_count = count_ref[dp]
-    my_owners = [owner_ref[dp, k] for k in range(capacity)]
+    my_owners = [owner_ref[k, 0, dp] for k in range(capacity)]
     picks = []
     for o in range(nd):
         pick = jnp.int32(0)
@@ -359,24 +471,23 @@
     for h in range(nd):
         sends = jnp.int32(0)
         for k in range(capacity):
-            sends = jnp.where((owner_ref[h, k] == dp) & (k < count_ref[h]), 1, sends)
+            sends = jnp.where((owner_ref[k, 0, h] == dp) & (k < count_ref[h]), 1, sends)
         for i in range(capacity):
             sources[i] = jnp.where((sends == 1) & (taken == i), h, sources[i])
         taken = taken + sends
 
-    relay(2, all_d, nz)
-    gather_wait(2, all_d)
+    both_wait(2, all_d)
     dy1 = flat_rows(all_d).astype(BF16)
     sent_a1[...] = times_transposed(dy1, down_ref[...]).astype(BF16)
     sum_start(4, sent_a1, got_a1)
     to_table(right_table, hidden_blocks, 1, dy1)
+    share_wait(9, mix_h1)
+    to_table(left_table, channel_blocks, 1, mix_h1[...])
 
     relay(3, all_f, nz)
     gather_wait(3, all_f)
-    f1 = flat_rows(all_f)
-    _, product_f1, squares_f1 = up_product(f1)
-    sent_f1[:, :hidden] = product_f1
-    sent_f1[:, hidden:] = squares_f1
+    _, *made = up_product(flat_rows(all_f))
+    stored_product(sent_f1, *made)
     sum_start(5, sent_f1, got_f1)
 
     total_a1 = sum_end(4, sent_a1, got_a1)
@@ -409,10 +520,15 @@
         block_copy(nz + (1 - 2 * (k % 2)) * ((k + 1) // 2)).start()
     loop(0, nd - 1, send_block)
 
-    reduce_start(2, normed_grad(mix_s1, all_b[:, :, 1].astype(F32).reshape(rows, width)), keep_b1, half_b1, other_b1)
+    def left_block(j):
+        block_copy(j).wait_send()
+    leaving.append(lambda: loop(1, nd, left_block))
+
+    reduce_start(2, normed_grad(mix_s1, rows_of(all_b, 1)), keep_b1, half_b1, other_b1)
     share_wait(11, mix_f1)
-    reduce_start(3, jnp.dot(mix_f1[...], down_ref[...], preferred_element_type=F32), keep_f1, half_f1, other_f1)
+    new_rows = jnp.dot(mix_f1[...], down_ref[...], preferred_element_type=F32)
     reduce_middle(2, keep_b1, half_b1, other_b1, chip_b1, rows_b1)
+    reduce_start(3, new_rows, keep_f1, half_f1, other_f1)
     reduce_middle(3, keep_f1, half_f1, other_f1, chip_f1, rows_f1)
     grads_ref[1] = (all_d[core, z].astype(F32) + reduce_end(2, chip_b1, rows_b1)).astype(BF16)
     outputs_ref[1] = (all_f[core, z].astype(F32) + reduce_end(3, chip_f1, rows_f1)).astype(BF16)
@@ -425,41 +541,31 @@
         ).wait_recv()
     loop(1, nd, got_block)
     for i in range(capacity):
-        owned_ref[i] = jnp.where(i < taken, recv_buf[sources[i]].astype(F32), 0.0)
+        owned_ref[i] = jnp.where(i < taken, recv_buf[sources[i]].astype(F32), 0.0).astype(BF16)
         filled_ref[i] = jnp.where(i < taken, jnp.ones((1, LANES), F32), 0.0)
 
-    for g, src, dst in ((0, src_a, all_a), (1, src_b, all_b)):
-        def left_gather(j, g=g, src=src, dst=dst):
-            gather_copy(g, src, dst, j, partner).wait_send()
-            relay_copy(g, dst, j).wait_send()
-        loop(1, nz, left_gather)
-        gather_copy(g, src, dst, nz, partner).wait_send()
-    for g, src, dst in ((2, src_d, all_d), (3, src_f, all_f)):
-        def left_next(j, g=g, src=src, dst=dst):
-            gather_copy(g, src, dst, j, partner).wait_send()
-            relay_copy(g, dst, j).wait_send()
-        loop(0, nz, left_next)
-    for g, sent, got in (
-        (0, sent_p0, got_p0), (1, sent_a0, got_a0), (2, sent_f0, got_f0),
-        (3, sent_p1, got_p1), (4, sent_a1, got_a1), (5, sent_f1, got_f1),
-    ):
-        for j in range(1, nt):
-            sum_copy(g, sent, got, j).wait_send()
-    for g, mix in ((6, mix_s0), (7, mix_f0), (8, mix_h0), (9, mix_h1), (10, mix_s1), (11, mix_f1)):
-        for j in range(1, nt):
-            share_copy(g, mix, j).wait_send()
-    for g, half, other, chip, got in (
-        (0, half_b0, other_b0, chip_b0, rows_b0), (1, half_f0, other_f0, chip_f0, rows_f0),
-        (2, half_b1, other_b1, chip_b1, rows_b1), (3, half_f1, other_f1, chip_f1, rows_f1),
-    ):
-        remote(half, other, reduce_send.at[g, 0], reduce_recv.at[g, 0], partner).wait_send()
-        def left_reduce(j, g=g, chip=chip, got=got):
-            chip_copy(g, chip, got, j).wait_send()
-        loop(1, nz, left_reduce)
-
-    def left_block(j):
-        block_copy(j).wait_send()
-    loop(1, nd, left_block)
+    for wait in leaving:
+        wait()
+
+
+def adam(
+    outputs_in, grads_in, owned_ref, filled_ref, first_ref, second_ref,
+    outputs_ref, grads_ref, first_out, second_out, direction_out,
+):
+    outputs_ref[...] = outputs_in[...]
+    grads_ref[...] = grads_in[...]
+    for i in range(owned_ref.shape[0]):
+        grad = owned_ref[i].astype(F32)
+        filled = filled_ref[i] > 0.5
+        first = 0.9 * first_ref[i] + 0.1 * grad
+        second = 0.999 * second_ref[i] + 0.001 * grad * grad
+        first_out[i] = jnp.where(filled, first, 0.0)
+        second_out[i] = jnp.where(filled, second, 0.0)
+        direction_out[i] = jnp.where(filled, first / (jnp.sqrt(second) + 1e-08), 0.0)
+
+
+def by_slot(lists):
+    return jnp.transpose(lists, (0, 3, 1, 2))[0]
 
 
 def body(
@@ -486,6 +592,7 @@
 
     scratch = [
         pltpu.VMEM((width, hidden), BF16), pltpu.VMEM((hidden, width), BF16),
+        *several(2, (local, width), BF16), pltpu.VMEM((1, width), BF16),
         *several(2, (2, local, width), BF16),
         *several(2, (2, nz, 2, local, width), BF16),
         *several(2, (local, width), BF16),
@@ -493,19 +600,20 @@
         *[pltpu.VMEM((rows, w), BF16) for w in (wide, hidden, wide, wide, hidden, wide)],
         *[pltpu.VMEM((nt, part, w), BF16) for w in (wide, hidden, wide, wide, hidden, wide)],
         *[pltpu.VMEM((rows, w), BF16) for w in (wide, hidden, hidden, hidden, wide, hidden)],
-        *several(4, (2, rows // 2, width), F32),
-        *several(4, (rows // 2, width), BF16),
-        *several(4, (rows // 2, width), BF16),
-        *several(4, (nz, local, width), BF16),
-        *several(4, (nz, local, width), BF16),
+        *several(3, (2, rows // 2, width), F32),
+        *several(3, (rows // 2, width), BF16),
+        *several(3, (rows // 2, width), BF16),
+        *several(3, (nz, local, width), BF16),
+        *several(3, (nz, local, width), BF16),
+        pltpu.VMEM((2, nz, local, width), BF16), pltpu.VMEM((nd, local, width), BF16),
         *several(2, (blocks, turns * rows, BLK), BF16),
         pltpu.VMEM((capacity, BLK, BLK), BF16),
         *several(2, (nd, BLK, BLK), BF16),
         pltpu.VMEM((part, hidden), F32), pltpu.VMEM((part, LANES), F32),
-        pltpu.SemaphoreType.DMA((2,)),
+        pltpu.SemaphoreType.DMA((2,)), pltpu.SemaphoreType.DMA((11,)),
         pltpu.SemaphoreType.DMA((4, 2 * nz)), pltpu.SemaphoreType.DMA((4, 2 * nz)),
         pltpu.SemaphoreType.DMA((12, nt)), pltpu.SemaphoreType.DMA((12, nt)),
-        pltpu.SemaphoreType.DMA((4, nz)), pltpu.SemaphoreType.DMA((4, nz)),
+        pltpu.SemaphoreType.DMA((4, 2 * nz)), pltpu.SemaphoreType.DMA((4, 2 * nz)),
         pltpu.SemaphoreType.DMA((nd,)), pltpu.SemaphoreType.DMA((nd,)),
     ]
     outputs, grads, owned, filled = pl.pallas_call(
@@ -513,10 +621,10 @@
         out_shape=(
             jax.ShapeDtypeStruct((turns, local, width), BF16),
             jax.ShapeDtypeStruct((turns, local, width), BF16),
-            jax.ShapeDtypeStruct((capacity, BLK, BLK), F32),
+            jax.ShapeDtypeStruct((capacity, BLK, BLK), BF16),
             jax.ShapeDtypeStruct((capacity, 1, LANES), F32),
         ),
-        in_specs=[smem] * 4 + [vmem] * 6 + [anywhere] * 2,
+        in_specs=[smem] * 4 + [anywhere] * 8,
         out_specs=[vmem] * 4,
         scratch_shapes=scratch,
         compiler_params=pltpu.CompilerParams(
@@ -524,17 +632,21 @@
         ),
         name="relay",
     )(
-        live_rows, held_blocks[0, 0], held_count[0, 0], held_owner[0, 0],
+        live_rows, by_slot(held_blocks), held_count[0, 0], by_slot(held_owner),
         section_inputs[0], entering[0], grad_outputs[0], arriving[0], stashed_inputs[0], norm_gain,
         up_weight[0], down_weight[0],
     )
-    is_filled = filled[:, :, :1] > 0.5
-    first_new = 0.9 * first_moment[0, 0, 0] + 0.1 * owned
-    second_new = 0.999 * second_moment[0, 0, 0] + 0.001 * owned * owned
-    direction = first_new / (jnp.sqrt(second_new) + 1e-08)
-    first_out = jnp.where(is_filled, first_new, 0.0)
-    second_out = jnp.where(is_filled, second_new, 0.0)
-    direction_out = jnp.where(is_filled, direction, 0.0)
+    block_shape = jax.ShapeDtypeStruct((capacity, BLK, BLK), F32)
+    outputs, grads, first_out, second_out, direction_out = pl.pallas_call(
+        adam,
+        out_shape=(
+            jax.ShapeDtypeStruct(outputs.shape, BF16), jax.ShapeDtypeStruct(grads.shape, BF16),
+            block_shape, block_shape, block_shape,
+        ),
+        in_specs=[vmem] * 6,
+        out_specs=[vmem] * 5,
+        name="adam",
+    )(outputs, grads, owned, filled, first_moment[0, 0, 0], second_moment[0, 0, 0])
     return (
         outputs[None], grads[None],
         first_out[None, None, None], second_out[None, None, None], direction_out[None, None, None],

time: 97.5 us -> 89.7 us (0.920); the launches traced: 96.1 us -> 89.3 us
  local copies, waits for them, and re-layouts: 3.95 us -> 0 us
  other arithmetic: 3.04 us -> 0 us
    squeeze x2 -> x0, local copies, waits for them, and re-layouts: 2.72 us -> none  [the longest x1 1.36 us: body(): held_blocks[0, 0]]
    pallas_call x0 -> x1, Pallas kernels: none -> 2.39 us  [body(): pl.pallas_call(adam, out_shape=(jax.ShapeDtypeStruct(outputs.shape, BF16)...]
    pallas_call x1, Pallas kernels: 87.8 us -> 85.6 us  [body(): pl.pallas_call(functools.partial(kernel, sizes), out_shape=(jax.ShapeDtyp...]
    broadcast_in_dim x1 -> x0, other arithmetic: 2.16 us -> none  [body(): direction_out[None, None, None]]
    unnamed x10 -> x0, local copies, waits for them, and re-layouts: 1.23 us -> none
where the time goes in v2:
time: 89.7 us; the launch traced here: 89.3 us
  Pallas kernels  88 us (98%)
  between operations  1.29 us (1%)
    pallas_call x1, Pallas kernels, body(): pl.pallas_call(functools.partial(kernel, sizes), out_shape=(jax.ShapeDtyp...  85.6 us
    pallas_call x1, Pallas kernels, body(): pl.pallas_call(adam, out_shape=(jax.ShapeDtypeStruct(outputs.shape, BF16)...  2.39 us

profile of v2, /device:TPU:1, one launch (start us, length us, event | category | flops | bytes accessed | tf_op | source)
XLA Modules:
  0.0 89.3 jit_solution(601982636180373460)
XLA Ops:
  1.3 85.6 %relay.1 = (bf16[2,8,640]{2,1,0:T(8,128)(2,1)}, bf16[2,8,640]{2,1,0:T(8,128)(2,1)}, bf16[6,128,128]{2,1,0:T(8,128)(2,1)}, f32[6,1,128]{2,1,0:T(1,128)}) custom-call(s32[1]{0:T(128)S(6)} %copy.19.live_ref, s32[6,1,16]{2,1,0:T(1,128)} %bitcast.30, s32[16]{0:T(128)} %bitcast.32, s32[6,1,16]{2,1,0:T(1,128)} %bitcast.31, bf16[8,640]{1,0:T(8,128)(2,1)} %bitcast.26, ...), custom_call_target="tpu_custom_call" | custom-call | tf_op jit(solution)/shard_map/relay/pallas_call | solution.py:619
  86.9 2.4 %adam.1 = (bf16[2,8,640]{2,1,0:T(8,128)(2,1)}, bf16[2,8,640]{2,1,0:T(8,128)(2,1)}, f32[6,128,128]{2,1,0:T(8,128)}, f32[6,128,128]{2,1,0:T(8,128)}, f32[6,128,128]{2,1,0:T(8,128)}) custom-call(bf16[2,8,640]{2,1,0:T(8,128)(2,1)} %get-tuple-element.14.outputs_in, bf16[2,8,640]{2,1,0:T(8,128)(2,1)} %get-tuple-element.15.grads_in, ...), custom_call_target="tpu_custom_call" | custom-call | tf_op jit(solution)/shard_map/adam/pallas_call | solution.py:640

commit v3 on v2

v3 whole, which is shorter than its diff:
```python
import functools

import jax
import jax.numpy as jnp
from jax import lax
from jax.experimental import pallas as pl
from jax.experimental.pallas import tpu as pltpu
from jax.sharding import PartitionSpec as P

MESH = pl.DeviceIdType.MESH
BLK = 128
LANES = 128
EPSILON = 1e-06
F32 = jnp.float32
BF16 = jnp.bfloat16


def times_transposed(left, right):
    return lax.dot_general(left, right, (((1,), (1,)), ((), ())), preferred_element_type=F32)


def lane_blocks_sum(value):
    total = value[:, :LANES]
    for start in range(LANES, value.shape[1], LANES):
        total = total + value[:, start : start + LANES]
    return total


def kernel(
    sizes,
    live_hbm, blocks_hbm, count_hbm, owner_hbm,
    section_hbm, entering_hbm, grad_hbm, arriving_hbm, stash_hbm, gain_hbm,
    up_hbm, down_hbm,
    outputs_ref, grads_ref, owned_ref, filled_ref,
    up_ref, down_ref,
    live_ref, blocks_ref, count_ref, owner_ref,
    entering_ref, arriving_ref, gain_ref,
    src_f, src_d,
    all_a, all_s, all_x, all_f, all_d,
    sent_p0, sent_a0, sent_f0, sent_p1, sent_a1, sent_f1,
    got_p0, got_a0, got_f0, got_p1, got_a1, got_f1,
    mix_s0, mix_h0, mix_f0, mix_h1, mix_s1, mix_f1,
    keep_f0, keep_b1, keep_f1,
    half_f0, half_b1, half_f1,
    other_f0, other_b1, other_f1,
    chip_f0, chip_b1, chip_f1,
    rows_f0, rows_b1, rows_f1,
    parts_b0, rows_b0,
    left_table, right_table, block_buf, send_buf, recv_buf,
    held_p1, held_scale1,
    weight_sem, input_sem,
    gather_send, gather_recv,
    tensor_send, tensor_recv,
    reduce_send, reduce_recv,
    block_send, block_recv,
):
    ns, nz, nt = sizes
    nd = 2 * nz
    local, width = entering_ref.shape
    hidden = up_ref.shape[1]
    rows = local * nd
    part = rows // nt
    dw = width * nt
    section = lax.axis_index("section")
    dp = lax.axis_index("dp")
    tensor = lax.axis_index("tensor")
    z = dp // 2
    core = dp % 2
    partner = (section, z * 2 + 1 - core, tensor)
    after = lax.rem(section + 1, ns)
    before = lax.rem(section + ns - 1, ns)

    leaving = []
    coming = {}

    def remote(src, dst, send_sem, recv_sem, device):
        return pltpu.make_async_remote_copy(
            src_ref=src, dst_ref=dst, send_sem=send_sem, recv_sem=recv_sem,
            device_id=device, device_id_type=MESH,
        )

    def far_first(k):
        return nz // 2 + (1 - 2 * (k % 2)) * ((k + 1) // 2)

    def zup(j):
        return lax.rem(z + j, nz)

    def zdown(j):
        return lax.rem(z + nz - j, nz)

    def tup(j):
        return lax.rem(tensor + j, nt)

    def loop(lo, hi, fn):
        def step(k, carry):
            fn(k)
            return carry
        lax.fori_loop(lo, hi, step, 0)

    weights_up = pltpu.make_async_copy(up_hbm, up_ref, weight_sem.at[0])
    weights_down = pltpu.make_async_copy(down_hbm, down_ref, weight_sem.at[1])

    barrier = pltpu.get_barrier_semaphore()

    def greet(device):
        pl.semaphore_signal(barrier, inc=1, device_id=device, device_id_type=MESH)

    def greet_dp(k):
        greet((section, lax.rem(dp + k, nd), tensor))

    def greet_sections(k):
        greet((after, k * 2 + core, tensor))
        greet((before, k * 2 + core, tensor))

    loop(1, nd, greet_dp)
    for j in range(1, nt):
        greet((section, dp, tup(j)))
    loop(0, nz, greet_sections)

    inputs = [
        pltpu.make_async_copy(src, dst, input_sem.at[i])
        for i, (src, dst) in enumerate((
            (stash_hbm.at[0], all_a.at[core, z, 0]), (grad_hbm, all_a.at[core, z, 1]),
            (section_hbm, all_s.at[core, z]), (stash_hbm.at[1], all_x.at[core, z]),
            (entering_hbm, entering_ref), (arriving_hbm, arriving_ref), (gain_hbm, gain_ref),
            (live_hbm, live_ref), (blocks_hbm, blocks_ref), (count_hbm, count_ref), (owner_hbm, owner_ref),
        ))
    ]
    for copy in inputs:
        copy.start()
    weights_up.start()
    weights_down.start()
    for copy in inputs:
        copy.wait()
    recv_buf[dp] = jnp.zeros(recv_buf.shape[1:], BF16)

    pl.semaphore_wait(barrier, (nd - 1) + (nt - 1) + 2 * nz)

    def together(ref, sends, receives):
        return remote(ref, ref, sends, receives, partner)

    def gather_start(g, src, dst, target_section, count):
        def send(k):
            j = far_first(k)
            remote(
                src, dst.at[core, z], gather_send.at[g, 0], gather_recv.at[g, 0],
                (target_section, zup(j) * 2 + core, tensor),
            ).start()
        loop(0, count, send)
        all_of = together(dst.at[0, :count], gather_send.at[g, 0], gather_recv.at[g, 0])
        leaving.append(all_of.wait_send)
        coming["gather", g] = all_of.wait_recv

    def relay(g, dst):
        coming.pop(("gather", g))()
        half = together(dst.at[core], gather_send.at[g, 1], gather_recv.at[g, 1])
        half.start()
        leaving.append(half.wait_send)
        coming["relay", g] = half.wait_recv

    def gather_wait(g):
        coming.pop(("relay", g))()

    def both_start(g, src, dst, target_section):
        def send(k):
            j = far_first(k)
            for other_core in range(2):
                remote(
                    src, dst.at[core, z], gather_send.at[g, 0], gather_recv.at[g, 0],
                    (target_section, zup(j) * 2 + lax.rem(core + other_core, 2), tensor),
                ).start()
        loop(0, nz, send)
        all_of = together(dst, gather_send.at[g, 0], gather_recv.at[g, 0])
        leaving.append(all_of.wait_send)
        coming["both", g] = all_of.wait_recv

    def both_wait(g):
        coming.pop(("both", g))()

    mine = pl.ds(pl.multiple_of(tensor * part, part), part)

    def sum_start(g, sent, got):
        for j in range(1, nt):
            remote(
                sent.at[pl.ds(pl.multiple_of(tup(j) * part, part), part)], got.at[j],
                tensor_send.at[g], tensor_recv.at[g], (section, dp, tup(j)),
            ).start()
        all_of = together(got.at[1:nt], tensor_send.at[g], tensor_recv.at[g])
        leaving.append(all_of.wait_send)
        coming["sum", g] = all_of.wait_recv

    def sum_end(g, sent, got):
        coming.pop(("sum", g))()
        total = sent[mine].astype(F32)
        for j in range(1, nt):
            total = total + got[j].astype(F32)
        return total

    def share_start(g, mix):
        for j in range(1, nt):
            remote(
                mix.at[mine], mix.at[mine], tensor_send.at[g], tensor_recv.at[g], (section, dp, tup(j))
            ).start()
        all_of = together(mix.at[: (nt - 1) * part], tensor_send.at[g], tensor_recv.at[g])
        leaving.append(all_of.wait_send)
        coming["share", g] = all_of.wait_recv

    def share_wait(g):
        coming.pop(("share", g))()

    def reduce_start(g, value, keep, half, other):
        keep[...] = value.reshape(2, rows // 2, width)
        half[...] = keep[1 - core].astype(BF16)
        swap = remote(half, other, reduce_send.at[g, 0], reduce_recv.at[g, 0], partner)
        swap.start()
        leaving.append(swap.wait_send)
        coming["swap", g] = swap.wait_recv

    def reduce_middle(g, keep, other, chip, got):
        coming.pop(("swap", g))()
        total = keep[core] + other[...].astype(F32)
        chip[...] = total.reshape(nz, local, width).astype(BF16)
        got[z] = chip[z]

        def send(k):
            j = far_first(k)
            remote(
                chip.at[zup(j)], got.at[z], reduce_send.at[g, 1], reduce_recv.at[g, 1],
                (section, zup(j) * 2 + core, tensor),
            ).start()
        loop(0, nz - 1, send)
        all_of = together(got.at[: nz - 1], reduce_send.at[g, 1], reduce_recv.at[g, 1])
        leaving.append(all_of.wait_send)
        coming["reduce", g] = all_of.wait_recv

    def reduce_end(g, got):
        coming.pop(("reduce", g))()
        return jnp.sum(got[...].astype(F32), axis=0)

    def scatter_start(g, value, parts, got):
        parts[...] = value.reshape(parts.shape).astype(BF16)
        got[dp] = parts[core, z]

        def send(j, other_core):
            target = lax.rem(core + other_core, 2)
            remote(
                parts.at[target, zup(j)], got.at[dp], reduce_send.at[g, 0], reduce_recv.at[g, 0],
                (section, zup(j) * 2 + target, tensor),
            ).start()

        def send_both(k):
            send(far_first(k), 0)
            send(far_first(k), 1)
        loop(0, nz - 1, send_both)
        send(0, 1)
        all_of = together(got.at[: nd - 1], reduce_send.at[g, 0], reduce_recv.at[g, 0])
        leaving.append(all_of.wait_send)
        coming["scatter", g] = all_of.wait_recv

    def scatter_end(g, got):
        coming.pop(("scatter", g))()
        return jnp.sum(got[...].astype(F32), axis=0)

    def flat_rows(ref):
        return ref[...].astype(F32).reshape(rows, width)

    gain = gain_ref[...].astype(F32)

    def scales_of(lane_squares):
        return lax.rsqrt(jnp.sum(lane_squares, axis=1, keepdims=True) / dw + EPSILON)

    def up_product(widened):
        normed = (widened * gain).astype(BF16)
        product = jnp.dot(normed, up_ref[...], preferred_element_type=F32)
        return normed, product.astype(BF16), lane_blocks_sum(widened * widened).astype(BF16)

    def to_table(table, first, turn, value):
        for b in range(value.shape[1] // BLK):
            table[first + b, turn * rows : (turn + 1) * rows, :] = value[:, b * BLK : (b + 1) * BLK]

    hidden_blocks = hidden // BLK
    channel_blocks = width // BLK

    def backward_middle(total_p, total_a, mix):
        product, scales = total_p
        inner = product * scales
        gate = jax.nn.sigmoid(inner)
        hidden_grad = total_a * gate * (1.0 + inner * (1.0 - gate))
        mix[mine, :hidden] = (hidden_grad * scales).astype(BF16)
        per_lane = lane_blocks_sum(hidden_grad * product)
        mix[mine, hidden:] = (per_lane * (scales * scales * scales / dw)).astype(BF16)

    def activated_of(product, scales):
        inner = product * scales
        return (inner * jax.nn.sigmoid(inner)).astype(BF16)

    def product_end(g, sent, got):
        total = sum_end(g, sent, got)
        return total[:, :hidden], scales_of(total[:, hidden:])

    def normed_grad(mix, widened):
        part_sum = times_transposed(mix[:, :hidden], up_ref[...])
        coefficient = jnp.sum(mix[:, hidden:].astype(F32), axis=1, keepdims=True)
        return part_sum * gain - coefficient * widened

    def stored_product(ref, product, lane_squares):
        ref[:, :hidden] = product
        ref[:, hidden:] = lane_squares

    def rows_of(ref, which):
        return ref[:, :, which].astype(F32).reshape(rows, width)

    gather_start(0, all_a.at[core, z], all_a, section, nz - 1)
    capacity = owner_ref.shape[0]
    up_count = hidden_blocks * channel_blocks
    left_index, right_index = [], []
    for k in range(capacity):
        number = blocks_ref[k, 0, dp]
        down_number = jnp.maximum(number - up_count, 0)
        is_up = number < up_count
        left_index.append(
            jnp.where(is_up, number // hidden_blocks, channel_blocks + down_number // channel_blocks)
        )
        right_index.append(
            jnp.where(is_up, number % hidden_blocks, hidden_blocks + down_number % channel_blocks)
        )
    my_count = count_ref[dp]
    my_owners = [owner_ref[k, 0, dp] for k in range(capacity)]
    picks = []
    for o in range(nd):
        pick = jnp.int32(0)
        for k in range(capacity):
            pick = jnp.where((my_owners[k] == o) & (k < my_count), k, pick)
        picks.append(pick)
    taken = jnp.int32(0)
    sources = [jnp.int32(0) for _ in range(capacity)]
    for h in range(nd):
        sends = jnp.int32(0)
        for k in range(capacity):
            sends = jnp.where((owner_ref[k, 0, h] == dp) & (k < count_ref[h]), 1, sends)
        for i in range(capacity):
            sources[i] = jnp.where((sends == 1) & (taken == i), h, sources[i])
        taken = taken + sends

    relay(0, all_a)
    gather_start(1, all_s.at[core, z], all_s, section, nz - 1)
    gather_start(4, all_x.at[core, z], all_x, section, nz - 1)
    weights_up.wait()
    gather_wait(0)
    normed0, *made = up_product(rows_of(all_a, 0))
    stored_product(sent_p0, *made)
    sum_start(0, sent_p0, got_p0)
    weights_down.wait()
    dy0 = rows_of(all_a, 1).astype(BF16)
    sent_a0[...] = times_transposed(dy0, down_ref[...]).astype(BF16)
    sum_start(1, sent_a0, got_a0)
    to_table(left_table, 0, 0, normed0)
    to_table(right_table, hidden_blocks, 0, dy0)

    relay(1, all_s)
    gather_wait(1)
    _, *made = up_product(flat_rows(all_s))
    stored_product(sent_f0, *made)

    total_p0 = product_end(0, sent_p0, got_p0)
    total_a0 = sum_end(1, sent_a0, got_a0)
    backward_middle(total_p0, total_a0, mix_s0)
    share_start(6, mix_s0)
    sum_start(2, sent_f0, got_f0)
    mix_h0[mine] = activated_of(*total_p0)

    relay(4, all_x)
    gather_wait(4)
    normed1, *made = up_product(flat_rows(all_x))
    stored_product(sent_p1, *made)
    to_table(left_table, 0, 1, normed1)

    share_wait(6)
    scatter_start(0, normed_grad(mix_s0, rows_of(all_a, 0)), parts_b0, rows_b0)
    sum_start(3, sent_p1, got_p1)
    to_table(right_table, 0, 0, mix_s0[:, :hidden])
    total_f0 = product_end(2, sent_f0, got_f0)
    mix_f0[mine] = activated_of(*total_f0)
    share_start(7, mix_f0)
    share_start(8, mix_h0)

    row_ids = dp * local + lax.broadcasted_iota(jnp.int32, (local, width), 0)
    masked = jnp.where(row_ids < live_ref[0], arriving_ref[...].astype(F32), 0.0)
    input_grad0 = all_a[core, z, 1].astype(F32) + scatter_end(0, rows_b0)
    src_d[...] = jnp.where(section == 0, masked, input_grad0).astype(BF16)
    both_start(2, src_d, all_d, before)
    grads_ref[0] = input_grad0.astype(BF16)

    total_p1, scales1 = product_end(3, sent_p1, got_p1)
    held_p1[...] = total_p1
    held_scale1[...] = jnp.broadcast_to(scales1, held_scale1.shape)
    mix_h1[mine] = activated_of(total_p1, scales1)
    share_start(9, mix_h1)
    share_wait(7)
    reduce_start(1, jnp.dot(mix_f0[...], down_ref[...], preferred_element_type=F32), keep_f0, half_f0, other_f0)
    reduce_middle(1, keep_f0, other_f0, chip_f0, rows_f0)
    share_wait(8)
    to_table(left_table, channel_blocks, 0, mix_h0[...])

    both_wait(2)
    dy1 = flat_rows(all_d).astype(BF16)
    sent_a1[...] = times_transposed(dy1, down_ref[...]).astype(BF16)
    sum_start(4, sent_a1, got_a1)
    to_table(right_table, hidden_blocks, 1, dy1)
    share_wait(9)
    to_table(left_table, channel_blocks, 1, mix_h1[...])

    output0 = all_s[core, z].astype(F32) + reduce_end(1, rows_f0)
    src_f[...] = jnp.where(section == ns - 1, entering_ref[...].astype(F32), output0).astype(BF16)
    both_start(3, src_f, all_f, after)
    outputs_ref[0] = output0.astype(BF16)

    total_a1 = sum_end(4, sent_a1, got_a1)
    backward_middle((held_p1[...], held_scale1[:, :1]), total_a1, mix_s1)
    share_start(10, mix_s1)

    share_wait(10)
    to_table(right_table, 0, 1, mix_s1[:, :hidden])
    for k in range(capacity):
        block = lax.dot_general(
            left_table[left_index[k]], right_table[right_index[k]],
            (((0,), (0,)), ((), ())), preferred_element_type=F32,
        )
        block_buf[k] = block.astype(BF16)
    for o in range(nd):
        send_buf[o] = block_buf[picks[o]]

    def send_block(k):
        owner = lax.rem(dp + nz + (1 - 2 * (k % 2)) * ((k + 1) // 2), nd)
        remote(
            send_buf.at[owner], recv_buf.at[dp], block_send.at[0], block_recv.at[0],
            (section, owner, tensor),
        ).start()
    loop(0, nd - 1, send_block)
    all_blocks = together(recv_buf.at[: nd - 1], block_send.at[0], block_recv.at[0])
    leaving.append(all_blocks.wait_send)
    coming["blocks", 0] = all_blocks.wait_recv

    both_wait(3)
    _, *made = up_product(flat_rows(all_f))
    stored_product(sent_f1, *made)
    sum_start(5, sent_f1, got_f1)

    reduce_start(2, normed_grad(mix_s1, flat_rows(all_x)), keep_b1, half_b1, other_b1)
    reduce_middle(2, keep_b1, other_b1, chip_b1, rows_b1)

    total_f1 = product_end(5, sent_f1, got_f1)
    mix_f1[mine] = activated_of(*total_f1)
    share_start(11, mix_f1)
    share_wait(11)
    reduce_start(3, jnp.dot(mix_f1[...], down_ref[...], preferred_element_type=F32), keep_f1, half_f1, other_f1)
    reduce_middle(3, keep_f1, other_f1, chip_f1, rows_f1)
    grads_ref[1] = (all_d[core, z].astype(F32) + reduce_end(2, rows_b1)).astype(BF16)
    outputs_ref[1] = (all_f[core, z].astype(F32) + reduce_end(3, rows_f1)).astype(BF16)

    coming.pop(("blocks", 0))()
    for i in range(capacity):
        owned_ref[i] = jnp.where(i < taken, recv_buf[sources[i]].astype(F32), 0.0).astype(BF16)
        filled_ref[i] = jnp.where(i < taken, jnp.ones((1, LANES), F32), 0.0)

    for wait in leaving:
        wait()


def adam(
    outputs_in, grads_in, owned_ref, filled_ref, first_ref, second_ref,
    outputs_ref, grads_ref, first_out, second_out, direction_out,
):
    outputs_ref[...] = outputs_in[...]
    grads_ref[...] = grads_in[...]
    for i in range(owned_ref.shape[0]):
        grad = owned_ref[i].astype(F32)
        filled = filled_ref[i] > 0.5
        first = 0.9 * first_ref[i] + 0.1 * grad
        second = 0.999 * second_ref[i] + 0.001 * grad * grad
        first_out[i] = jnp.where(filled, first, 0.0)
        second_out[i] = jnp.where(filled, second, 0.0)
        direction_out[i] = jnp.where(filled, first / (jnp.sqrt(second) + 1e-08), 0.0)


def by_slot(lists):
    return jnp.transpose(lists, (0, 3, 1, 2))[0]


def body(
    sizes,
    section_inputs, entering, grad_outputs, arriving, live_rows, stashed_inputs, norm_gain,
    up_weight, down_weight, held_blocks, held_count, held_owner, first_moment, second_moment,
):
    ns, nz, nt = sizes
    nd = 2 * nz
    local, width = section_inputs.shape[1:]
    hidden = up_weight.shape[2]
    rows = local * nd
    part = rows // nt
    capacity = held_owner.shape[3]
    turns = stashed_inputs.shape[1]
    blocks = hidden // BLK + width // BLK
    vmem = pl.BlockSpec(memory_space=pltpu.VMEM)
    anywhere = pl.BlockSpec(memory_space=pl.ANY)
    wide = hidden + LANES

    def several(count, shape, dtype):
        return [pltpu.VMEM(shape, dtype) for _ in range(count)]

    scratch = [
        pltpu.VMEM((width, hidden), BF16), pltpu.VMEM((hidden, width), BF16),
        pltpu.SMEM((1,), jnp.int32), pltpu.SMEM((capacity, 1, nd), jnp.int32),
        pltpu.SMEM((nd,), jnp.int32), pltpu.SMEM((capacity, 1, nd), jnp.int32),
        *several(2, (local, width), BF16), pltpu.VMEM((1, width), BF16),
        *several(2, (local, width), BF16),
        pltpu.VMEM((2, nz, 2, local, width), BF16),
        *several(4, (2, nz, local, width), BF16),
        *[pltpu.VMEM((rows, w), BF16) for w in (wide, hidden, wide, wide, hidden, wide)],
        *[pltpu.VMEM((nt, part, w), BF16) for w in (wide, hidden, wide, wide, hidden, wide)],
        *[pltpu.VMEM((rows, w), BF16) for w in (wide, hidden, hidden, hidden, wide, hidden)],
        *several(3, (2, rows // 2, width), F32),
        *several(3, (rows // 2, width), BF16),
        *several(3, (rows // 2, width), BF16),
        *several(3, (nz, local, width), BF16),
        *several(3, (nz, local, width), BF16),
        pltpu.VMEM((2, nz, local, width), BF16), pltpu.VMEM((nd, local, width), BF16),
        *several(2, (blocks, turns * rows, BLK), BF16),
        pltpu.VMEM((capacity, BLK, BLK), BF16),
        *several(2, (nd, BLK, BLK), BF16),
        pltpu.VMEM((part, hidden), F32), pltpu.VMEM((part, LANES), F32),
        pltpu.SemaphoreType.DMA((2,)), pltpu.SemaphoreType.DMA((11,)),
        pltpu.SemaphoreType.DMA((5, 2)), pltpu.SemaphoreType.DMA((5, 2)),
        pltpu.SemaphoreType.DMA((12,)), pltpu.SemaphoreType.DMA((12,)),
        pltpu.SemaphoreType.DMA((4, 2)), pltpu.SemaphoreType.DMA((4, 2)),
        pltpu.SemaphoreType.DMA((1,)), pltpu.SemaphoreType.DMA((1,)),
    ]
    outputs, grads, owned, filled = pl.pallas_call(
        functools.partial(kernel, sizes),
        out_shape=(
            jax.ShapeDtypeStruct((turns, local, width), BF16),
            jax.ShapeDtypeStruct((turns, local, width), BF16),
            jax.ShapeDtypeStruct((capacity, BLK, BLK), BF16),
            jax.ShapeDtypeStruct((capacity, 1, LANES), F32),
        ),
        in_specs=[anywhere] * 12,
        out_specs=[vmem] * 4,
        scratch_shapes=scratch,
        compiler_params=pltpu.CompilerParams(
            collective_id=0, has_side_effects=True, vmem_limit_bytes=56 * 1024 * 1024
        ),
        name="relay",
    )(
        live_rows, by_slot(held_blocks), held_count[0, 0], by_slot(held_owner),
        section_inputs[0], entering[0], grad_outputs[0], arriving[0], stashed_inputs[0], norm_gain,
        up_weight[0], down_weight[0],
    )
    block_shape = jax.ShapeDtypeStruct((capacity, BLK, BLK), F32)
    outputs, grads, first_out, second_out, direction_out = pl.pallas_call(
        adam,
        out_shape=(
            jax.ShapeDtypeStruct(outputs.shape, BF16), jax.ShapeDtypeStruct(grads.shape, BF16),
            block_shape, block_shape, block_shape,
        ),
        in_specs=[vmem] * 6,
        out_specs=[vmem] * 5,
        name="adam",
    )(outputs, grads, owned, filled, first_moment[0, 0, 0], second_moment[0, 0, 0])
    return (
        outputs[None], grads[None],
        first_out[None, None, None], second_out[None, None, None], direction_out[None, None, None],
    )


def solution(mesh):
    sizes = (mesh.shape["section"], mesh.shape["dp"] // 2, mesh.shape["tensor"])
    return jax.shard_map(
        functools.partial(body, sizes),
        mesh=mesh,
        in_specs=(
            P("section", "dp", "tensor"),
            P(None, "dp", "tensor"),
            P("section", "dp", "tensor"),
            P(None, "dp", "tensor"),
            P(),
            P("section", None, "dp", "tensor"),
            P("section", "tensor"),
            P("section", "tensor", "dp"),
            P("section", "dp", "tensor"),
            P("section", "tensor", None, None),
            P("section", "tensor", None),
            P("section", "tensor", None, None),
            P("section", "tensor", "dp", None, None, None),
            P("section", "tensor", "dp", None, None, None),
        ),
        out_specs=(
            P("section", None, "dp", "tensor"),
            P("section", None, "dp", "tensor"),
            P("section", "tensor", "dp", None, None, None),
            P("section", "tensor", "dp", None, None, None),
            P("section", "tensor", "dp", None, None, None),
        ),
        check_vma=False,
    )
```

time: 89.7 us -> 81.6 us (0.910)
  Pallas kernels: 88 us -> 79.2 us
    pallas_call x1, Pallas kernels: 85.6 us -> 76.8 us  [body(): pl.pallas_call(functools.partial(kernel, sizes), out_shape=(jax.ShapeDtyp...]
where the time goes in v3:
time: 81.6 us; the launch traced here: 80.5 us
  Pallas kernels  79.2 us (97%)
  between operations  1.29 us (2%)
    pallas_call x1, Pallas kernels, body(): pl.pallas_call(functools.partial(kernel, sizes), out_shape=(jax.ShapeDtyp...  76.8 us
    pallas_call x1, Pallas kernels, body(): pl.pallas_call(adam, out_shape=(jax.ShapeDtypeStruct(outputs.shape, BF16)...  2.39 us

profile of v3, /device:TPU:1, one launch (start us, length us, event | category | flops | bytes accessed | tf_op | source)
XLA Modules:
  0.0 80.5 jit_solution(15097838724404090278)
XLA Ops:
  1.3 76.8 %relay.1 = (bf16[2,8,640]{2,1,0:T(8,128)(2,1)}, bf16[2,8,640]{2,1,0:T(8,128)(2,1)}, bf16[6,128,128]{2,1,0:T(8,128)(2,1)}, f32[6,1,128]{2,1,0:T(1,128)}) custom-call(s32[1]{0:T(128)S(6)} %copy.19.live_hbm, s32[6,1,16]{2,1,0:T(1,128)} %bitcast.30, s32[16]{0:T(128)} %bitcast.32, s32[6,1,16]{2,1,0:T(1,128)} %bitcast.31, bf16[8,640]{1,0:T(8,128)(2,1)} %bitcast.26, ...), custom_call_target="tpu_custom_call" | custom-call | tf_op jit(solution)/shard_map/relay/pallas_call | solution.py:538
  78.1 2.4 %adam.1 = (bf16[2,8,640]{2,1,0:T(8,128)(2,1)}, bf16[2,8,640]{2,1,0:T(8,128)(2,1)}, f32[6,128,128]{2,1,0:T(8,128)}, f32[6,128,128]{2,1,0:T(8,128)}, f32[6,128,128]{2,1,0:T(8,128)}) custom-call(bf16[2,8,640]{2,1,0:T(8,128)(2,1)} %get-tuple-element.14.outputs_in, bf16[2,8,640]{2,1,0:T(8,128)(2,1)} %get-tuple-element.15.grads_in, ...), custom_call_target="tpu_custom_call" | custom-call | tf_op jit(solution)/shard_map/adam/pallas_call | solution.py:559

commit v4 on v3

--- a/solution.py
+++ b/solution.py
@@ -105,17 +105,15 @@
     def greet(device):
         pl.semaphore_signal(barrier, inc=1, device_id=device, device_id_type=MESH)
 
-    def greet_dp(k):
-        greet((section, lax.rem(dp + k, nd), tensor))
-
-    def greet_sections(k):
-        greet((after, k * 2 + core, tensor))
-        greet((before, k * 2 + core, tensor))
-
-    loop(1, nd, greet_dp)
+    def greet_z(k):
+        greet((section, zup(far_first(k)) * 2 + core, tensor))
+
+    loop(0, nz - 1, greet_z)
+    greet(partner)
     for j in range(1, nt):
         greet((section, dp, tup(j)))
-    loop(0, nz, greet_sections)
+    greet((after, dp, tensor))
+    greet((before, dp, tensor))
 
     inputs = [
         pltpu.make_async_copy(src, dst, input_sem.at[i])
@@ -134,7 +132,7 @@
         copy.wait()
     recv_buf[dp] = jnp.zeros(recv_buf.shape[1:], BF16)
 
-    pl.semaphore_wait(barrier, (nd - 1) + (nt - 1) + 2 * nz)
+    pl.semaphore_wait(barrier, nz + (nt - 1) + 2)
 
     def together(ref, sends, receives):
         return remote(ref, ref, sends, receives, partner)
@@ -179,29 +177,30 @@
 
     mine = pl.ds(pl.multiple_of(tensor * part, part), part)
 
-    def sum_start(g, sent, got):
+    def sum_start(g, sent, got, columns=slice(None)):
         for j in range(1, nt):
             remote(
-                sent.at[pl.ds(pl.multiple_of(tup(j) * part, part), part)], got.at[j],
+                sent.at[pl.ds(pl.multiple_of(tup(j) * part, part), part), columns], got.at[j, :, columns],
                 tensor_send.at[g], tensor_recv.at[g], (section, dp, tup(j)),
             ).start()
-        all_of = together(got.at[1:nt], tensor_send.at[g], tensor_recv.at[g])
+        all_of = together(got.at[1:nt, :, columns], tensor_send.at[g], tensor_recv.at[g])
         leaving.append(all_of.wait_send)
         coming["sum", g] = all_of.wait_recv
 
-    def sum_end(g, sent, got):
+    def sum_end(g, sent, got, columns=slice(None)):
         coming.pop(("sum", g))()
-        total = sent[mine].astype(F32)
+        total = sent[mine, columns].astype(F32)
         for j in range(1, nt):
-            total = total + got[j].astype(F32)
+            total = total + got[j, :, columns].astype(F32)
         return total
 
-    def share_start(g, mix):
+    def share_start(g, mix, columns=slice(None)):
         for j in range(1, nt):
             remote(
-                mix.at[mine], mix.at[mine], tensor_send.at[g], tensor_recv.at[g], (section, dp, tup(j))
+                mix.at[mine, columns], mix.at[mine, columns],
+                tensor_send.at[g], tensor_recv.at[g], (section, dp, tup(j)),
             ).start()
-        all_of = together(mix.at[: (nt - 1) * part], tensor_send.at[g], tensor_recv.at[g])
+        all_of = together(mix.at[: (nt - 1) * part, columns], tensor_send.at[g], tensor_recv.at[g])
         leaving.append(all_of.wait_send)
         coming["share", g] = all_of.wait_recv
 
@@ -269,10 +268,26 @@
     def scales_of(lane_squares):
         return lax.rsqrt(jnp.sum(lane_squares, axis=1, keepdims=True) / dw + EPSILON)
 
-    def up_product(widened):
-        normed = (widened * gain).astype(BF16)
-        product = jnp.dot(normed, up_ref[...], preferred_element_type=F32)
-        return normed, product.astype(BF16), lane_blocks_sum(widened * widened).astype(BF16)
+    cut = hidden // LANES // 2 * LANES
+    hidden_parts = (slice(0, cut), slice(cut, hidden))
+    product_parts = (slice(0, LANES + cut), slice(LANES + cut, LANES + hidden))
+    mix_parts = (slice(0, cut), slice(cut, hidden + LANES))
+
+    def normed_of(widened, sent):
+        sent[:, :LANES] = lane_blocks_sum(widened * widened).astype(BF16)
+        return (widened * gain).astype(BF16)
+
+    def product_of(normed, sent):
+        sent[:, LANES:] = jnp.dot(normed, up_ref[...], preferred_element_type=F32).astype(BF16)
+
+    def product_part(normed, sent, i):
+        columns = hidden_parts[i]
+        product = jnp.dot(normed, up_ref[:, columns], preferred_element_type=F32)
+        sent[:, LANES + columns.start : LANES + columns.stop] = product.astype(BF16)
+
+    def act_grad_part(grads, sent, i):
+        columns = hidden_parts[i]
+        sent[:, columns] = times_transposed(grads, down_ref[columns, :]).astype(BF16)
 
     def to_table(table, first, turn, value):
         for b in range(value.shape[1] // BLK):
@@ -281,13 +296,14 @@
     hidden_blocks = hidden // BLK
     channel_blocks = width // BLK
 
-    def backward_middle(total_p, total_a, mix):
-        product, scales = total_p
+    def backward_part(product, scales, act_grad, mix, i):
         inner = product * scales
         gate = jax.nn.sigmoid(inner)
-        hidden_grad = total_a * gate * (1.0 + inner * (1.0 - gate))
-        mix[mine, :hidden] = (hidden_grad * scales).astype(BF16)
-        per_lane = lane_blocks_sum(hidden_grad * product)
+        hidden_grad = act_grad * gate * (1.0 + inner * (1.0 - gate))
+        mix[mine, hidden_parts[i]] = (hidden_grad * scales).astype(BF16)
+        return lane_blocks_sum(hidden_grad * product)
+
+    def scale_part(per_lane, scales, mix):
         mix[mine, hidden:] = (per_lane * (scales * scales * scales / dw)).astype(BF16)
 
     def activated_of(product, scales):
@@ -296,16 +312,15 @@
 
     def product_end(g, sent, got):
         total = sum_end(g, sent, got)
-        return total[:, :hidden], scales_of(total[:, hidden:])
-
-    def normed_grad(mix, widened):
-        part_sum = times_transposed(mix[:, :hidden], up_ref[...])
+        return total[:, LANES:], scales_of(total[:, :LANES])
+
+    def normed_grad_part(mix, i):
+        columns = hidden_parts[i]
+        return times_transposed(mix[:, columns], up_ref[:, columns])
+
+    def row_grads(part_sum, mix, widened):
         coefficient = jnp.sum(mix[:, hidden:].astype(F32), axis=1, keepdims=True)
         return part_sum * gain - coefficient * widened
-
-    def stored_product(ref, product, lane_squares):
-        ref[:, :hidden] = product
-        ref[:, hidden:] = lane_squares
 
     def rows_of(ref, which):
         return ref[:, :, which].astype(F32).reshape(rows, width)
@@ -347,36 +362,49 @@
     gather_start(4, all_x.at[core, z], all_x, section, nz - 1)
     weights_up.wait()
     gather_wait(0)
-    normed0, *made = up_product(rows_of(all_a, 0))
-    stored_product(sent_p0, *made)
-    sum_start(0, sent_p0, got_p0)
+    normed0 = normed_of(rows_of(all_a, 0), sent_p0)
+    product_part(normed0, sent_p0, 0)
+    sum_start(0, sent_p0, got_p0, product_parts[0])
     weights_down.wait()
     dy0 = rows_of(all_a, 1).astype(BF16)
-    sent_a0[...] = times_transposed(dy0, down_ref[...]).astype(BF16)
-    sum_start(1, sent_a0, got_a0)
+    act_grad_part(dy0, sent_a0, 0)
+    sum_start(1, sent_a0, got_a0, hidden_parts[0])
+    product_part(normed0, sent_p0, 1)
+    sum_start(12, sent_p0, got_p0, product_parts[1])
+    act_grad_part(dy0, sent_a0, 1)
+    sum_start(13, sent_a0, got_a0, hidden_parts[1])
     to_table(left_table, 0, 0, normed0)
     to_table(right_table, hidden_blocks, 0, dy0)
 
     relay(1, all_s)
     gather_wait(1)
-    _, *made = up_product(flat_rows(all_s))
-    stored_product(sent_f0, *made)
-
-    total_p0 = product_end(0, sent_p0, got_p0)
-    total_a0 = sum_end(1, sent_a0, got_a0)
-    backward_middle(total_p0, total_a0, mix_s0)
-    share_start(6, mix_s0)
+    product_of(normed_of(flat_rows(all_s), sent_f0), sent_f0)
+
+    total_p0 = sum_end(0, sent_p0, got_p0, product_parts[0])
+    scales0 = scales_of(total_p0[:, :LANES])
+    first_p0 = total_p0[:, LANES:]
+    total_a0 = sum_end(1, sent_a0, got_a0, hidden_parts[0])
+    per_lane = backward_part(first_p0, scales0, total_a0, mix_s0, 0)
+    share_start(6, mix_s0, mix_parts[0])
+    last_p0 = sum_end(12, sent_p0, got_p0, product_parts[1])
+    total_a0 = sum_end(13, sent_a0, got_a0, hidden_parts[1])
+    scale_part(per_lane + backward_part(last_p0, scales0, total_a0, mix_s0, 1), scales0, mix_s0)
+    share_start(14, mix_s0, mix_parts[1])
     sum_start(2, sent_f0, got_f0)
-    mix_h0[mine] = activated_of(*total_p0)
+    mix_h0[mine, hidden_parts[0]] = activated_of(first_p0, scales0)
+    mix_h0[mine, hidden_parts[1]] = activated_of(last_p0, scales0)
 
     relay(4, all_x)
     gather_wait(4)
-    normed1, *made = up_product(flat_rows(all_x))
-    stored_product(sent_p1, *made)
+    normed1 = normed_of(flat_rows(all_x), sent_p1)
+    product_of(normed1, sent_p1)
     to_table(left_table, 0, 1, normed1)
 
     share_wait(6)
-    scatter_start(0, normed_grad(mix_s0, rows_of(all_a, 0)), parts_b0, rows_b0)
+    part_sum = normed_grad_part(mix_s0, 0)
+    share_wait(14)
+    part_sum = part_sum + normed_grad_part(mix_s0, 1)
+    scatter_start(0, row_grads(part_sum, mix_s0, rows_of(all_a, 0)), parts_b0, rows_b0)
     sum_start(3, sent_p1, got_p1)
     to_table(right_table, 0, 0, mix_s0[:, :hidden])
     total_f0 = product_end(2, sent_f0, got_f0)
@@ -404,8 +432,10 @@
 
     both_wait(2)
     dy1 = flat_rows(all_d).astype(BF16)
-    sent_a1[...] = times_transposed(dy1, down_ref[...]).astype(BF16)
-    sum_start(4, sent_a1, got_a1)
+    act_grad_part(dy1, sent_a1, 0)
+    sum_start(4, sent_a1, got_a1, hidden_parts[0])
+    act_grad_part(dy1, sent_a1, 1)
+    sum_start(15, sent_a1, got_a1, hidden_parts[1])
     to_table(right_table, hidden_blocks, 1, dy1)
     share_wait(9)
     to_table(left_table, channel_blocks, 1, mix_h1[...])
@@ -415,12 +445,19 @@
     both_start(3, src_f, all_f, after)
     outputs_ref[0] = output0.astype(BF16)
 
-    total_a1 = sum_end(4, sent_a1, got_a1)
-    backward_middle((held_p1[...], held_scale1[:, :1]), total_a1, mix_s1)
-    share_start(10, mix_s1)
+    scales1 = held_scale1[:, :1]
+    total_a1 = sum_end(4, sent_a1, got_a1, hidden_parts[0])
+    per_lane = backward_part(held_p1[:, hidden_parts[0]], scales1, total_a1, mix_s1, 0)
+    share_start(10, mix_s1, mix_parts[0])
+    total_a1 = sum_end(15, sent_a1, got_a1, hidden_parts[1])
+    per_lane = per_lane + backward_part(held_p1[:, hidden_parts[1]], scales1, total_a1, mix_s1, 1)
+    scale_part(per_lane, scales1, mix_s1)
+    share_start(16, mix_s1, mix_parts[1])
 
     share_wait(10)
-    to_table(right_table, 0, 1, mix_s1[:, :hidden])
+    to_table(right_table, 0, 1, mix_s1[:, :cut])
+    share_wait(16)
+    to_table(right_table, cut // BLK, 1, mix_s1[:, cut:hidden])
     for k in range(capacity):
         block = lax.dot_general(
             left_table[left_index[k]], right_table[right_index[k]],
@@ -442,11 +479,11 @@
     coming["blocks", 0] = all_blocks.wait_recv
 
     both_wait(3)
-    _, *made = up_product(flat_rows(all_f))
-    stored_product(sent_f1, *made)
+    product_of(normed_of(flat_rows(all_f), sent_f1), sent_f1)
     sum_start(5, sent_f1, got_f1)
 
-    reduce_start(2, normed_grad(mix_s1, flat_rows(all_x)), keep_b1, half_b1, other_b1)
+    part_sum = normed_grad_part(mix_s1, 0) + normed_grad_part(mix_s1, 1)
+    reduce_start(2, row_grads(part_sum, mix_s1, flat_rows(all_x)), keep_b1, half_b1, other_b1)
     reduce_middle(2, keep_b1, other_b1, chip_b1, rows_b1)
 
     total_f1 = product_end(5, sent_f1, got_f1)
@@ -531,7 +568,7 @@
         pltpu.VMEM((part, hidden), F32), pltpu.VMEM((part, LANES), F32),
         pltpu.SemaphoreType.DMA((2,)), pltpu.SemaphoreType.DMA((11,)),
         pltpu.SemaphoreType.DMA((5, 2)), pltpu.SemaphoreType.DMA((5, 2)),
-        pltpu.SemaphoreType.DMA((12,)), pltpu.SemaphoreType.DMA((12,)),
+        pltpu.SemaphoreType.DMA((17,)), pltpu.SemaphoreType.DMA((17,)),
         pltpu.SemaphoreType.DMA((4, 2)), pltpu.SemaphoreType.DMA((4, 2)),
         pltpu.SemaphoreType.DMA((1,)), pltpu.SemaphoreType.DMA((1,)),
     ]

time: 81.6 us -> 78.8 us (0.966)
  Pallas kernels: 79.2 us -> 77.1 us
    pallas_call x1, Pallas kernels: 76.8 us -> 74.8 us  [body(): pl.pallas_call(functools.partial(kernel, sizes), out_shape=(jax.ShapeDtyp...]
where the time goes in v4:
time: 78.8 us; the launch traced here: 78.4 us
  Pallas kernels  77.1 us (98%)
  between operations  1.29 us (2%)
    pallas_call x1, Pallas kernels, body(): pl.pallas_call(functools.partial(kernel, sizes), out_shape=(jax.ShapeDtyp...  74.8 us
    pallas_call x1, Pallas kernels, body(): pl.pallas_call(adam, out_shape=(jax.ShapeDtypeStruct(outputs.shape, BF16)...  2.39 us

profile of v4, /device:TPU:1, one launch (start us, length us, event | category | flops | bytes accessed | tf_op | source)
XLA Modules:
  0.0 78.4 jit_solution(15312309174805401338)
XLA Ops:
  1.3 74.8 %relay.1 = (bf16[2,8,640]{2,1,0:T(8,128)(2,1)}, bf16[2,8,640]{2,1,0:T(8,128)(2,1)}, bf16[6,128,128]{2,1,0:T(8,128)(2,1)}, f32[6,1,128]{2,1,0:T(1,128)}) custom-call(s32[1]{0:T(128)S(6)} %copy.19.live_hbm, s32[6,1,16]{2,1,0:T(1,128)} %bitcast.30, s32[16]{0:T(128)} %bitcast.32, s32[6,1,16]{2,1,0:T(1,128)} %bitcast.31, bf16[8,640]{1,0:T(8,128)(2,1)} %bitcast.26, ...), custom_call_target="tpu_custom_call" | custom-call | tf_op jit(solution)/shard_map/relay/pallas_call | solution.py:575
  76.0 2.4 %adam.1 = (bf16[2,8,640]{2,1,0:T(8,128)(2,1)}, bf16[2,8,640]{2,1,0:T(8,128)(2,1)}, f32[6,128,128]{2,1,0:T(8,128)}, f32[6,128,128]{2,1,0:T(8,128)}, f32[6,128,128]{2,1,0:T(8,128)}) custom-call(bf16[2,8,640]{2,1,0:T(8,128)(2,1)} %get-tuple-element.14.outputs_in, bf16[2,8,640]{2,1,0:T(8,128)(2,1)} %get-tuple-element.15.grads_in, ...), custom_call_target="tpu_custom_call" | custom-call | tf_op jit(solution)/shard_map/adam/pallas_call | solution.py:596

commit v5 on v4

--- a/solution.py
+++ b/solution.py
@@ -31,7 +31,7 @@
     live_hbm, blocks_hbm, count_hbm, owner_hbm,
     section_hbm, entering_hbm, grad_hbm, arriving_hbm, stash_hbm, gain_hbm,
     up_hbm, down_hbm,
-    outputs_ref, grads_ref, owned_ref, filled_ref,
+    outputs_ref, grads_ref, owned_hbm, filled_hbm,
     up_ref, down_ref,
     live_ref, blocks_ref, count_ref, owner_ref,
     entering_ref, arriving_ref, gain_ref,
@@ -47,7 +47,7 @@
     rows_f0, rows_b1, rows_f1,
     parts_b0, rows_b0,
     left_table, right_table, block_buf, send_buf, recv_buf,
-    held_p1, held_scale1,
+    held_p1, held_scale1, early_blocks, owned_ref, filled_ref, out_sem,
     weight_sem, input_sem,
     gather_send, gather_recv,
     tensor_send, tensor_recv,
@@ -305,6 +305,12 @@
 
     def scale_part(per_lane, scales, mix):
         mix[mine, hidden:] = (per_lane * (scales * scales * scales / dw)).astype(BF16)
+
+    def block_of(k, turn_rows):
+        return lax.dot_general(
+            left_table[left_index[k], turn_rows], right_table[right_index[k], turn_rows],
+            (((0,), (0,)), ((), ())), preferred_element_type=F32,
+        )
 
     def activated_of(product, scales):
         inner = product * scales
@@ -413,7 +419,7 @@
     share_start(8, mix_h0)
 
     row_ids = dp * local + lax.broadcasted_iota(jnp.int32, (local, width), 0)
-    masked = jnp.where(row_ids < live_ref[0], arriving_ref[...].astype(F32), 0.0)
+    masked = jnp.where(row_ids < live_ref[0, 0, 0], arriving_ref[...].astype(F32), 0.0)
     input_grad0 = all_a[core, z, 1].astype(F32) + scatter_end(0, rows_b0)
     src_d[...] = jnp.where(section == 0, masked, input_grad0).astype(BF16)
     both_start(2, src_d, all_d, before)
@@ -454,16 +460,14 @@
     scale_part(per_lane, scales1, mix_s1)
     share_start(16, mix_s1, mix_parts[1])
 
+    for k in range(capacity):
+        early_blocks[k] = block_of(k, slice(0, rows))
     share_wait(10)
     to_table(right_table, 0, 1, mix_s1[:, :cut])
     share_wait(16)
     to_table(right_table, cut // BLK, 1, mix_s1[:, cut:hidden])
     for k in range(capacity):
-        block = lax.dot_general(
-            left_table[left_index[k]], right_table[right_index[k]],
-            (((0,), (0,)), ((), ())), preferred_element_type=F32,
-        )
-        block_buf[k] = block.astype(BF16)
+        block_buf[k] = (early_blocks[k] + block_of(k, slice(rows, 2 * rows))).astype(BF16)
     for o in range(nd):
         send_buf[o] = block_buf[picks[o]]
 
@@ -492,13 +496,20 @@
     share_wait(11)
     reduce_start(3, jnp.dot(mix_f1[...], down_ref[...], preferred_element_type=F32), keep_f1, half_f1, other_f1)
     reduce_middle(3, keep_f1, other_f1, chip_f1, rows_f1)
-    grads_ref[1] = (all_d[core, z].astype(F32) + reduce_end(2, rows_b1)).astype(BF16)
-    outputs_ref[1] = (all_f[core, z].astype(F32) + reduce_end(3, rows_f1)).astype(BF16)
-
     coming.pop(("blocks", 0))()
     for i in range(capacity):
         owned_ref[i] = jnp.where(i < taken, recv_buf[sources[i]].astype(F32), 0.0).astype(BF16)
         filled_ref[i] = jnp.where(i < taken, jnp.ones((1, LANES), F32), 0.0)
+    blocks_out = (
+        pltpu.make_async_copy(owned_ref, owned_hbm, out_sem.at[0]),
+        pltpu.make_async_copy(filled_ref, filled_hbm, out_sem.at[1]),
+    )
+    for copy in blocks_out:
+        copy.start()
+    grads_ref[1] = (all_d[core, z].astype(F32) + reduce_end(2, rows_b1)).astype(BF16)
+    outputs_ref[1] = (all_f[core, z].astype(F32) + reduce_end(3, rows_f1)).astype(BF16)
+    for copy in blocks_out:
+        copy.wait()
 
     for wait in leaving:
         wait()
@@ -547,7 +558,7 @@
 
     scratch = [
         pltpu.VMEM((width, hidden), BF16), pltpu.VMEM((hidden, width), BF16),
-        pltpu.SMEM((1,), jnp.int32), pltpu.SMEM((capacity, 1, nd), jnp.int32),
+        pltpu.SMEM((1, 1, 1), jnp.int32), pltpu.SMEM((capacity, 1, nd), jnp.int32),
         pltpu.SMEM((nd,), jnp.int32), pltpu.SMEM((capacity, 1, nd), jnp.int32),
         *several(2, (local, width), BF16), pltpu.VMEM((1, width), BF16),
         *several(2, (local, width), BF16),
@@ -566,6 +577,9 @@
         pltpu.VMEM((capacity, BLK, BLK), BF16),
         *several(2, (nd, BLK, BLK), BF16),
         pltpu.VMEM((part, hidden), F32), pltpu.VMEM((part, LANES), F32),
+        pltpu.VMEM((capacity, BLK, BLK), F32),
+        pltpu.VMEM((capacity, BLK, BLK), BF16), pltpu.VMEM((capacity, 1, LANES), F32),
+        pltpu.SemaphoreType.DMA((2,)),
         pltpu.SemaphoreType.DMA((2,)), pltpu.SemaphoreType.DMA((11,)),
         pltpu.SemaphoreType.DMA((5, 2)), pltpu.SemaphoreType.DMA((5, 2)),
         pltpu.SemaphoreType.DMA((17,)), pltpu.SemaphoreType.DMA((17,)),
@@ -581,14 +595,14 @@
             jax.ShapeDtypeStruct((capacity, 1, LANES), F32),
         ),
         in_specs=[anywhere] * 12,
-        out_specs=[vmem] * 4,
+        out_specs=[vmem] * 2 + [anywhere] * 2,
         scratch_shapes=scratch,
         compiler_params=pltpu.CompilerParams(
             collective_id=0, has_side_effects=True, vmem_limit_bytes=56 * 1024 * 1024
         ),
         name="relay",
     )(
-        live_rows, by_slot(held_blocks), held_count[0, 0], by_slot(held_owner),
+        live_rows.reshape(1, 1, 1), by_slot(held_blocks), held_count[0, 0], by_slot(held_owner),
         section_inputs[0], entering[0], grad_outputs[0], arriving[0], stashed_inputs[0], norm_gain,
         up_weight[0], down_weight[0],
     )

time: 78.8 us -> 78.7 us (level)
  no operation moved by 1% of the time
where the time goes in v5:
time: 78.7 us; the launch traced here: 78.4 us
  Pallas kernels  77.1 us (98%)
  between operations  1.29 us (2%)
    pallas_call x1, Pallas kernels, body(): pl.pallas_call(functools.partial(kernel, sizes), out_shape=(jax.ShapeDtyp...  74.7 us
    pallas_call x1, Pallas kernels, body(): pl.pallas_call(adam, out_shape=(jax.ShapeDtypeStruct(outputs.shape, BF16)...  2.39 us

profile of v5, /device:TPU:1, one launch (start us, length us, event | category | flops | bytes accessed | tf_op | source)
XLA Modules:
  0.0 78.4 jit_solution(4894100082391613506)
XLA Ops:
  1.3 74.7 %relay.1 = (bf16[2,8,640]{2,1,0:T(8,128)(2,1)}, bf16[2,8,640]{2,1,0:T(8,128)(2,1)}, bf16[6,128,128]{2,1,0:T(8,128)(2,1)}, f32[6,1,128]{2,1,0:T(1,128)}) custom-call(s32[1,1,1]{2,1,0:T(1,128)} %bitcast.22.live_hbm, s32[6,1,16]{2,1,0:T(1,128)} %bitcast.32, s32[16]{0:T(128)} %bitcast.34, s32[6,1,16]{2,1,0:T(1,128)} %bitcast.33, bf16[8,640]{1,0:T(8,128)(2,1)} %bitcast.28, ...), custom_call_target="tpu_custom_call" | custom-call | tf_op jit(solution)/shard_map/relay/pallas_call | solution.py:589
  76.0 2.4 %adam.1 = (bf16[2,8,640]{2,1,0:T(8,128)(2,1)}, bf16[2,8,640]{2,1,0:T(8,128)(2,1)}, f32[6,128,128]{2,1,0:T(8,128)}, f32[6,128,128]{2,1,0:T(8,128)}, f32[6,128,128]{2,1,0:T(8,128)}) custom-call(bf16[2,8,640]{2,1,0:T(8,128)(2,1)} %get-tuple-element.14.outputs_in, bf16[2,8,640]{2,1,0:T(8,128)(2,1)} %get-tuple-element.15.grads_in, ...), custom_call_target="tpu_custom_call" | custom-call | tf_op jit(solution)/shard_map/adam/pallas_call | solution.py:610
